TPU v7x, 32 devices: a whole 2x2x4 slice. The times are simulated.
32 devices in a mesh: dp: 8 (over z, x), seq: 4 (over y, core).
Axes of the slice: x: 2, y: 2, z: 4, core: 2. Of those that a mesh axis runs over, the one named last changes fastest.
Arguments:
- inputs: bfloat16 [32, 1024, 1024], P('dp', 'seq'), may hold values from -6 to 6
- norm_gain: float32 [1024], replicated, may hold values from 0.1 to 1.9
- norm_shift: float32 [1024], replicated, may hold values from -3 to 3
- qkv_weight: bfloat16 [1024, 3072], replicated, may hold values from -0.1875 to 0.1875
- out_weight: bfloat16 [1024, 1024], replicated, may hold values from -0.75 to 0.75
- up_weight: bfloat16 [1024, 4096], replicated, may hold values from -0.1875 to 0.1875
- up_bias: float32 [4096], replicated, may hold values from -3 to 3
- down_weight: bfloat16 [4096, 1024], replicated, may hold values from -0.09375 to 0.09375
- down_bias: float32 [1024], replicated, may hold values from -3 to 3
- partners: int32 [32], P('dp'), may hold values from 0 to 31, as said below
- families: int32 [32, 1024], P('dp'), may hold values from 0 to 1023, as said below
- cotangent: bfloat16 [32, 1024, 1024], P('dp', 'seq'), may hold values from -6 to 6
Outputs:
- layer_out: bfloat16 [32, 1024, 1024], P('dp', 'seq')
- input_grad: float32 [32, 1024, 1024], P('dp', 'seq')
- gain_grad: float32 [1024], replicated
- shift_grad: float32 [1024], replicated
- qkv_grad: float32 [1024, 3072], P('dp', 'seq')
- out_grad: float32 [1024, 1024], P('dp', 'seq')
- up_grad: float32 [1024, 4096], P('dp', 'seq')
- up_bias_grad: float32 [4096], replicated
- down_grad: float32 [4096, 1024], P('dp', 'seq')
- down_bias_grad: float32 [1024], replicated
Inputs may be any that keep to these rules, and one draw needn't show every extreme that they name: partners pairs the rows of each aligned block of 4 rows two by two: partners[partners[r]] = r, partners[r] != r, and partners[r] lies in the block of r. `families`: family ids never fall along a row and the last position of every row has id 1024 - 1; in each aligned block of 4 rows at least one row is a single group over all 1024 positions.
All inputs are finite; a program needn't handle non-finite values.
Results may differ from a plain program's by a relative error of at most 0.0099.
Values may be sent and summed in bfloat16 or wider, within the bound.
A program may use at most 256 MiB of HBM per device.

v0:
```python
import functools

import jax
import jax.numpy as jnp
import numpy as np
from jax import lax
from jax.experimental import pallas as pl
from jax.experimental.pallas import tpu as pltpu
from jax.sharding import PartitionSpec as P

F32 = jnp.float32
BF16 = jnp.bfloat16
HEAD_DIM = 64
ROT = 32
EPS = 1e-05
C0 = 0.7978845608028654
C1 = C0 * 0.044715
TILE = 256
FF_SPLITS = (0, 176, 80), (96, 112, 48)
AT_SPLIT = 96, 112, 48
EARLY_SPLIT = 48, 64, 16
TAIL_SPLITS = (0, 80, 48), (0, 48, 16), (0, 32, 32)
FF_TICKS = (6, 9, 15, 18, 22), (12, 15, 20, 22, 24)
AT_TICKS = (0, 2, 7, 10, 14), (4, 7, 12, 15, 19), (13, 15, 19, 21, 24)
ORDER = ((0, 3), (4, 7), (1, 2), (5, 6))
MESH_ID = pl.DeviceIdType.MESH
ANYWHERE = pl.BlockSpec(memory_space=pl.ANY)
DMA = pltpu.SemaphoreType.DMA


def dot(a, b):
    return lax.dot_general(a, b, (((1,), (0,)), ((), ())), preferred_element_type=F32)


def dot_nt(a, b):
    return lax.dot_general(a, b, (((1,), (1,)), ((), ())), preferred_element_type=F32)


def dot_tn(a, b):
    return lax.dot_general(a, b, (((0,), (0,)), ((), ())), preferred_element_type=F32)


def whole(shape):
    return pl.BlockSpec(shape, lambda p: (0,) * len(shape), pipeline_mode=pl.Buffered(1))


def pick(step, values):
    out = jnp.int32(values[0])
    for i, value in enumerate(values[1:], 1):
        out = jnp.where(step == i, value, out)
    return out


def normalize(values):
    centered = values - jnp.mean(values, -1, keepdims=True)
    scale = lax.rsqrt(jnp.mean(centered * centered, -1, keepdims=True) + EPS)
    return centered * scale, scale


def each_band(count, body):
    def step(m, carry):
        body(pl.ds(pl.multiple_of(m * 256, 256), 256), m)
        return carry

    lax.fori_loop(0, count, step, 0)


def local_copy(src, dst, sem):
    return pltpu.make_async_copy(src, dst, sem)


def remote_copy(src, dst, send, recv, to):
    return pltpu.make_async_remote_copy(src_ref=src, dst_ref=dst, send_sem=send, recv_sem=recv, device_id=to,
                                        device_id_type=MESH_ID)


class Place:
    def __init__(self):
        self.dp, self.seq = lax.axis_index("dp"), lax.axis_index("seq")
        self.z, self.x, self.y, self.c = self.dp // 2, self.dp % 2, self.seq // 2, self.seq % 2
        self.twin = (self.dp, self.y * 2 + 1 - self.c)
        self.beside_y = (self.dp, (1 - self.y) * 2 + self.c)
        self.across = (self.dp, (1 - self.y) * 2 + 1 - self.c)
        self.beside_x = (self.z * 2 + 1 - self.x, self.seq)
        self.along_z = [(((self.z + j) % 4) * 2 + self.x, self.seq) for j in (1, 2, 3)]
        self.peers = [((self.seq + j) % 4, (self.dp, (self.seq + j) % 4)) for j in (1, 2, 3)]
        self.partners = [self.twin, self.beside_y, self.beside_x] + self.along_z

    def greet(self):
        barrier = pltpu.get_barrier_semaphore()
        for partner in self.partners + [self.across]:
            pl.semaphore_signal(barrier, inc=1, device_id=partner, device_id_type=MESH_ID)
        pl.semaphore_wait(barrier, len(self.partners) + 1)


def add_into(dst, src, lead):
    rows, w = src.shape[-2:]
    band = rows
    while band * w > 65536 and band % 32 == 0:
        band //= 2
    count = 1
    for n in lead:
        count *= n

    def body(t, carry):
        block, part = t // (rows // band), t % (rows // band)
        index = []
        for n in reversed(lead):
            index.insert(0, block % n)
            block = block // n
        at = tuple(index) + (pl.ds(pl.multiple_of(part * band, band), band), slice(None))
        dst[at] = dst[at] + src[at]
        return carry

    lax.fori_loop(0, count * (rows // band), body, 0)


def piece_scratch(w, split):
    ra, rb, rc = split
    r = sum(split)
    out = [((2, 4, 2, r), 1), ((2, 4, 2, r), 1), ((4, 2, ra), ra), ((2, 4, rb), rb), ((3, 2, 2, rc), rc), ((4, ra), ra), ((4, rb), rb), ((2, rc), rc),
           ((3, ra + rb), ra + rb), ((rc,), rc)]
    return [pltpu.VMEM(shape + (w,), BF16) for shape, used in out if used] + [DMA((14,)), DMA((14,)), DMA((2,))]


def piece_count(split):
    return len(piece_scratch(128, split))


class Piece:
    def __init__(self, place, part, done, split, scratch):
        self.p, self.part, self.done, self.split = place, part, done, split
        ra, rb, rc = split
        names = [("a", 1), ("from_twin", 1), ("ya", ra), ("xb", rb), ("zc", rc), ("xa", ra), ("yb", rb), ("xc", rc), ("zab", ra + rb), ("yc", rc)]
        scratch = list(scratch)
        for name, used in names:
            setattr(self, name, scratch.pop(0) if used else None)
        self.ss, self.rs, self.ls = scratch
        self.rows_a, self.rows_b, self.rows_ab, self.rows_c = pl.ds(0, ra), pl.ds(ra, rb), pl.ds(0, ra + rb), pl.ds(ra + rb, rc)

    def copies(self, stage):
        p, a, (ra, rb, rc) = self.p, self.a, self.split
        out = []
        slot = (0, 2, 7, 10)[stage]

        def send(src, dst, to):
            k = slot + len(out)
            out.append(remote_copy(src, dst, self.ss.at[k], self.rs.at[k], to))

        zs = [((p.z + 1 + j) % 4, p.along_z[j]) for j in range(3)]
        if stage == 0:
            for k in (0, 1):
                send(self.part(k, 1 - p.c), self.from_twin.at[k], p.twin)
        if stage == 1:
            if ra:
                send(a.at[1 - p.y, :, :, self.rows_a, :], self.ya, p.beside_y)
            if rb:
                send(a.at[:, :, 1 - p.x, self.rows_b, :], self.xb, p.beside_x)
            for j in range(3 if rc else 0):
                send(a.at[:, zs[j][0], :, self.rows_c, :], self.zc.at[j], zs[j][1])
        if stage == 2:
            if ra:
                send(a.at[p.y, :, 1 - p.x, self.rows_a, :], self.xa, p.beside_x)
            if rb:
                send(a.at[1 - p.y, :, p.x, self.rows_b, :], self.yb, p.beside_y)
            if rc:
                send(a.at[:, p.z, 1 - p.x, self.rows_c, :], self.xc, p.beside_x)
        if stage == 3:
            for j in range(3 if ra + rb else 0):
                send(a.at[p.y, zs[j][0], p.x, self.rows_ab, :], self.zab.at[j], zs[j][1])
            if rc:
                send(a.at[1 - p.y, p.z, p.x, self.rows_c, :], self.yc, p.beside_y)
        return out

    def own(self):
        return [local_copy(self.part(k, self.p.c), self.a.at[k], self.ls.at[k]) for k in (0, 1)]

    def tick(self, t):
        p, a, (ra, rb, rc) = self.p, self.a, self.split
        if t > 0:
            for copy in self.copies(t - 1):
                copy.wait()
        if t == 0:
            for copy in self.copies(0) + self.own():
                copy.start()
        if t == 1:
            for copy in self.own():
                copy.wait()
            add_into(a, self.from_twin, (2, 4, 2))
        if t == 2:
            if ra:
                add_into(a.at[p.y, :, :, self.rows_a, :], self.ya, (4, 2))
            if rb:
                add_into(a.at[:, :, p.x, self.rows_b, :], self.xb, (2, 4))
            for j in range(3 if rc else 0):
                add_into(a.at[:, p.z, :, self.rows_c, :], self.zc.at[j], (2, 2))
        if t == 3:
            if ra:
                add_into(a.at[p.y, :, p.x, self.rows_a, :], self.xa, (4,))
            if rb:
                add_into(a.at[p.y, :, p.x, self.rows_b, :], self.yb, (4,))
            if rc:
                add_into(a.at[:, p.z, p.x, self.rows_c, :], self.xc, (2,))
        if t in (1, 2, 3):
            for copy in self.copies(t):
                copy.start()
        if t == 4:
            mine = a.at[p.y, p.z, p.x]
            parts = []
            if ra + rb:
                total = mine[self.rows_ab, :].astype(F32)
                for j in range(3):
                    total += self.zab[j].astype(F32)
                parts.append(total)
            if rc:
                parts.append(mine[self.rows_c, :].astype(F32) + self.yc[...].astype(F32))
            self.done(jnp.concatenate(parts, 0) if len(parts) > 1 else parts[0])


def ff_kernel(inp_ref, g_ref, gain_ref, shift_ref, bias_ref, wu_ref, wd_ref, *rest, linked):
    hand, rest = (rest[:2], rest[2:]) if linked else ((), rest)
    y_ref, dn_ref, sums_ref, ub_ref = rest[:4]
    outs, rest = (rest[4:11], rest[11:]) if linked else (rest[4:6], rest[6:])
    x_s, xt_s, act_s, dh_s, wu_s, wd_s, gu_s, gd_s, wu_sem, wd_sem, gu_sem, gd_sem = rest[:12]
    rest = rest[12:]
    step = pl.program_id(0)
    last = pl.num_programs(0) - 1
    n, d = x_s.shape
    hidden = bias_ref.shape[1]
    group = hidden // 8
    tile = 512
    slot = step % 2

    def places(at):
        k, j = at // 2, at % 2
        return [(s, (2 * s + j) * group + k * 128) for s in range(4)]

    def weights(at, slot):
        out = []
        for s, f in places(at):
            f = pl.multiple_of(f, 128)
            out.append(local_copy(wu_ref.at[:, pl.ds(f, 128)], wu_s.at[slot, :, pl.ds(s * 128, 128)], wu_sem.at[slot, s]))
            out.append(local_copy(wd_ref.at[pl.ds(f, 128), :], wd_s.at[slot, pl.ds(s * 128, 128), :], wd_sem.at[slot, s]))
        return out

    def results(at):
        out = []
        k, j = at // 2, at % 2
        for s, f in places(at):
            f = pl.multiple_of(f, 128)
            up, down = gu_s.at[:, :, :, pl.ds(s * 128, 128)], gd_s.at[pl.ds(s * 128, 128), :]
            if linked:
                col = pl.multiple_of(s * 256 + j * 128, 128)
                to = outs[0].at[k, :, :, pl.ds(0, 128), pl.ds(col, 128)], outs[0].at[k, s, j, pl.ds(128, 128), :]
            else:
                to = outs[0].at[:, :, :, pl.ds(f, 128)], outs[1].at[pl.ds(f, 128), :]
            out.append(local_copy(up, to[0], gu_sem.at[s]))
            out.append(local_copy(down, to[1], gd_sem.at[s]))
        return out

    if linked:
        place = Place()
        row_send, row_recv, own_sem = rest[:3]
        rest = rest[3:]

        def swaps():
            out = []
            for a in range(2):
                for j, (to, device) in enumerate(place.peers):
                    out.append(remote_copy(hand[a].at[to], outs[1 + a].at[place.seq], row_send.at[a, j], row_recv.at[a, j], device))
                out.append(local_copy(hand[a].at[place.seq], outs[1 + a].at[place.seq], own_sem.at[a]))
            return out

        def part_of(k):
            return lambda y, c: outs[0].at[k, :, :, :, pl.ds(pl.multiple_of((y * 2 + c) * 256, 256), 256)]

        def done_at(k):
            def done(total):
                outs[3 + 2 * k][...] = total[0:128]
                outs[4 + 2 * k][...] = total[128:256]
            return done

        cut = piece_count(FF_SPLITS[0])
        made = [Piece(place, part_of(k), done_at(k), FF_SPLITS[k], (rest[:cut], rest[cut:])[k]) for k in range(2)]

    def tick(position):
        for which, times in enumerate(FF_TICKS if linked else ()):
            for t, at in enumerate(times):
                if min(at // 3, 7) * 3 + position == at:
                    pl.when(step == min(at // 3, 7))(functools.partial(made[which].tick, t))

    @pl.when(step == 0)
    def _():
        for copy in weights(0, 0):
            copy.start()
        if linked:
            place.greet()
            for copy in swaps():
                copy.start()
        sums_ref[...] = jnp.zeros_like(sums_ref)

        @functools.partial(each_band, n // 256)
        def _(rows, m):
            xhat, _ = normalize(inp_ref[rows, :].astype(F32))
            normed = (xhat * gain_ref[...] + shift_ref[...]).astype(BF16)
            x_s[rows, :] = normed
            xt_s[:, rows] = normed.T
            sums_ref[2:3, :] += jnp.sum(g_ref[rows, :].astype(F32), 0, keepdims=True)

    @pl.when(step > 0)
    def _():
        for copy in results(step - 1):
            copy.wait()

    tick(0)

    @pl.when(step < last)
    def _():
        for copy in weights(step + 1, 1 - slot):
            copy.start()
    for copy in weights(step, slot):
        copy.wait()
    w_up, w_down = wu_s.at[slot], wd_s.at[slot]
    bias = jnp.concatenate([bias_ref[:, pl.ds(pl.multiple_of(f, 128), 128)] for _, f in places(step)], 1)
    unit_sums = None
    for m in range(n // tile):
        here = slice(m * tile, (m + 1) * tile)
        v = dot(x_s[here, :], w_up[...]) + bias
        vv = v * v
        a = 0.5 + 0.5 * jnp.tanh(v * (C0 + C1 * vv))
        act = v * a
        slope = a + act * (1.0 - a) * (2 * C0 + 6 * C1 * vv)
        act_s[here, :] = act.astype(BF16)
        dh = (dot_nt(g_ref[here, :], w_down[...]) * slope).astype(BF16)
        dh_s[here, :] = dh
        total = jnp.sum(dh.astype(F32), 0, keepdims=True)
        unit_sums = total if unit_sums is None else unit_sums + total
    for s, f in places(step):
        ub_ref[:, pl.ds(pl.multiple_of(f, 128), 128)] = unit_sums[:, s * 128:(s + 1) * 128]

    tick(1)
    for m in range(d // 256):
        grads = dot(xt_s[m * 256:(m + 1) * 256, :], dh_s[...]).astype(BF16)
        gu_s[m, 0] = grads[0:128]
        gu_s[m, 1] = grads[128:256]
    gd_s[...] = dot_tn(act_s[...], g_ref[...]).astype(BF16)
    for copy in results(step):
        copy.start()
    tick(2)
    for m in range(n // tile):
        here = slice(m * tile, (m + 1) * tile)
        y = dot(act_s[here, :], w_down[...])
        dn = dot_nt(dh_s[here, :], w_up[...])

        @pl.when(step == 0)
        def _():
            y_ref[here, :] = y
            dn_ref[here, :] = dn

        @pl.when(step > 0)
        def _():
            y_ref[here, :] += y
            dn_ref[here, :] += dn

    tick(3)

    @pl.when(step == last)
    def _():
        @functools.partial(each_band, n // 256)
        def _(here, m):
            total = dn_ref[here, :]
            xhat, _ = normalize(inp_ref[here, :].astype(F32))
            sums_ref[0:1, :] += jnp.sum(total * xhat, 0, keepdims=True)
            sums_ref[1:2, :] += jnp.sum(total, 0, keepdims=True)

        for copy in results(step):
            copy.wait()
        if linked:
            for copy in swaps():
                copy.wait()


def feed_forward(inp, g, gain, shift, bias, wu, wd, linked):
    rows, span, d = inp.shape
    n, hidden = rows * span, bias.shape[0]
    sd, vm = jax.ShapeDtypeStruct, pltpu.VMEM
    out_shape = [sd((n, d), F32), sd((n, d), F32), sd((8, d), F32), sd((1, hidden), F32)]
    out_specs = [whole((n, d)), whole((n, d)), whole((8, d)), whole((1, hidden))]
    scratch = [vm((n, d), BF16), vm((d, n), BF16), vm((n, 512), BF16), vm((n, 512), BF16), vm((2, d, 512), BF16), vm((2, 512, d), BF16),
               vm((4, 2, 128, 512), BF16), vm((512, d), BF16), DMA((2, 4)), DMA((2, 4)), DMA((4,)), DMA((4,))]
    more, params = [], {}
    if linked:
        more = [inp, g]
        out_shape += [sd((4, 4, 2, 256, d), BF16), sd(inp.shape, BF16), sd(inp.shape, BF16), *[sd((128, 256), F32)] * 4]
        out_specs += [ANYWHERE] * 3 + [whole((128, 256))] * 4
        scratch += [DMA((2, 3)), DMA((2, 3)), DMA((2,))] + piece_scratch(256, FF_SPLITS[0]) + piece_scratch(256, FF_SPLITS[1])
        params = dict(collective_id=0, has_side_effects=True)
    else:
        out_shape += [sd((4, 2, 128, hidden), BF16), sd((hidden, d), BF16)]
        out_specs += [ANYWHERE] * 2
    return pl.pallas_call(
        functools.partial(ff_kernel, linked=linked), out_shape=out_shape, grid=(hidden // 512,),
        in_specs=[whole((n, d)), whole((n, d)), whole((1, d)), whole((1, d)), whole((1, hidden)), ANYWHERE, ANYWHERE] + [ANYWHERE] * len(more),
        out_specs=out_specs, scratch_shapes=scratch,
        compiler_params=pltpu.CompilerParams(vmem_limit_bytes=58 * 2**20, **params),
        cost_estimate=pl.CostEstimate(flops=52_000_000_000, bytes_accessed=50_000_000, transcendentals=4_000_000),
    )(inp.reshape(n, d), g.reshape(n, d), gain.reshape(1, d), shift.reshape(1, d), bias.reshape(1, hidden), wu, wd, *more)


def turn(x, c, s, sign):
    lanes = x.shape[1]
    lane = lax.broadcasted_iota(jnp.int32, x.shape, 1) % HEAD_DIM
    other = jnp.where(lane < ROT // 2, pltpu.roll(x, lanes - ROT // 2, 1), pltpu.roll(x, ROT // 2, 1))
    return x * c + (sign * other) * s


def tile_place(tile):
    early = [kind * 8 + pair for two in ORDER[:2] for pair in two for kind in range(3)]
    block = tile // 6
    mates = sorted(t for t in range(24) if t // 6 == block and (t in early) == (tile in early))
    return block, mates.index(tile)


def attn_kernel(raw_ref, g_ref, gain_ref, shift_ref, fam_ref, tab_ref, wqkv_ref, wo_ref, *rest, linked):
    hand, rest = (rest[:1], rest[1:]) if linked else ((), rest)
    dn_ref, sums_ref, gqkv_ref, go_ref, heads_ref = rest[:5]
    outs, rest = (rest[5:10], rest[10:]) if linked else ((), rest[5:])
    (x_s, xt_s, c_s, s_s, w_s, wo_s, q_s, k_s, v_s, do_s, kt_s, vt_s, ht_s, dqt_s, dk_s, dv_s, draw_s, dn_s, gq_s, go_s, heads_s,
     famr_s, famc_s, w_sem, wo_sem, gq_sem, go_sem, h_sem) = rest[:28]
    rest = rest[28:]
    step = pl.program_id(0)
    steps = len(ORDER)
    last = steps - 1
    n, d = raw_ref.shape
    lanes = 256
    pairs = d // 128
    slot = step % 2

    def weights(at, slot):
        out = []
        for half in range(2):
            pair = pick(at, [o[half] for o in ORDER])
            for kind in range(3):
                col = pl.multiple_of((kind * pairs + pair) * 128, 128)
                j = kind * 2 + half
                out.append(local_copy(wqkv_ref.at[:, pl.ds(col, 128)], w_s.at[slot, :, pl.ds(j * 128, 128)], w_sem.at[slot, j]))
            row = pl.multiple_of(pair * 128, 128)
            out.append(local_copy(wo_ref.at[pl.ds(row, 128), :], wo_s.at[slot, pl.ds(half * 128, 128), :], wo_sem.at[slot, half]))
        return out

    def results(at):
        out = []
        for half in range(2):
            pair = pick(at, [o[half] for o in ORDER])
            for kind in range(3):
                j = kind * 2 + half
                if linked:
                    col = pick(at, [block * 384 + rank * 128 for block, rank in (tile_place(kind * 8 + o[half]) for o in ORDER)])
                    to = gqkv_ref.at[at // 2, :, :, :, pl.ds(pl.multiple_of(col, 128), 128)]
                else:
                    to = gqkv_ref.at[:, :, :, pl.ds(pl.multiple_of((kind * pairs + pair) * 128, 128), 128)]
                out.append(local_copy(gq_s.at[:, :, :, pl.ds(j * 128, 128)], to, gq_sem.at[j]))
            out.append(local_copy(go_s.at[pl.ds(half * 128, 128), :], go_ref.at[pair // 2, pair % 2], go_sem.at[half]))
        return out

    if linked:
        place = Place()
        head_send, head_recv = rest[:2]
        rest = rest[2:]

        def heads_out(at):
            cols = pl.ds(pl.multiple_of(at * lanes, lanes), lanes)
            span = n // 4
            out = []
            for j, (to, device) in enumerate(place.peers):
                src = heads_s.at[pl.ds(pl.multiple_of(to * span, span), span), :]
                out.append(remote_copy(src, heads_ref.at[place.seq, :, cols], head_send.at[at, j], head_recv.at[at, j], device))
            mine = heads_s.at[pl.ds(pl.multiple_of(place.seq * span, span), span), :]
            return out, local_copy(mine, heads_ref.at[place.seq, :, cols], h_sem.at[0])

        def part_of(source, k, w):
            return lambda y, c: source.at[k, :, :, :, pl.ds(pl.multiple_of((y * 2 + c) * w, 128), w)]

        def done_at(k):
            def done(total):
                if k == 2:
                    outs[4][...] = total
                else:
                    outs[2 * k][...] = total[0:128]
                    outs[2 * k + 1][...] = total[128:256]
            return done

        cut = piece_count(AT_SPLIT)
        made = [Piece(place, part_of(hand[0], 2, 256), done_at(0), AT_SPLIT, rest[:cut]),
                Piece(place, part_of(hand[0], 3, 256), done_at(1), AT_SPLIT, rest[cut:2 * cut]),
                Piece(place, part_of(gqkv_ref, 0, 384), done_at(2), EARLY_SPLIT, rest[2 * cut:])]
        plan = {}
        for which, times in enumerate(AT_TICKS):
            for t, at in enumerate(times):
                plan.setdefault(at, []).append((which, t))
    else:
        plan = {}

    def tick(position):
        for at, what in sorted(plan.items()):
            if min(at // 6, last) * 6 + position == at:
                def run(what=what):
                    for which, t in sorted(what, key=lambda w: (-w[1], w[0])):
                        made[which].tick(t)
                pl.when(step == min(at // 6, last))(run)

    @pl.when(step == 0)
    def _():
        for copy in weights(0, 0):
            copy.start()
        if linked:
            place.greet()

    @pl.when(step > 0)
    def _():
        for copy in results(step - 1):
            copy.wait()

    tick(0)

    @pl.when(step == 0)
    def _():
        family = fam_ref[pl.ds(lax.axis_index("seq"), 1), :].astype(F32)
        famr_s[...] = family
        for m in range(n // 128):
            rows = slice(m * 128, m * 128 + 128)
            famc_s[rows, :] = jnp.broadcast_to(family[:, rows], (128, 128)).T
        for a in range(n // 32):
            rows = slice(a * 32, a * 32 + 32)
            ca, sa = tab_ref[0, a:a + 1, :], tab_ref[1, a:a + 1, :]
            cb, sb = tab_ref[2], tab_ref[3]
            c1 = ca * cb - sa * sb
            s1 = sa * cb + ca * sb
            lane = lax.broadcasted_iota(jnp.int32, c1.shape, 1) % HEAD_DIM
            c_s[rows, :] = jnp.where(lane < ROT, c1, 1.0)
            s_s[rows, :] = jnp.where(lane < ROT // 2, -s1, jnp.where(lane < ROT, s1, 0.0))
        @functools.partial(each_band, n // 256)
        def _(rows, m):
            xhat, _ = normalize(raw_ref[rows, :].astype(F32))
            normed = (xhat * gain_ref[...] + shift_ref[...]).astype(BF16)
            x_s[rows, :] = normed
            xt_s[:, rows] = normed.T

    @pl.when(step < last)
    def _():
        for copy in weights(step + 1, 1 - slot):
            copy.start()
    for copy in weights(step, slot):
        copy.wait()

    w_ref, wo1_ref = w_s.at[slot], wo_s.at[slot]
    scaling = HEAD_DIM ** -0.5

    def both(rows):
        c, s = c_s[rows, :], s_s[rows, :]
        return jnp.concatenate([c, c], 1), jnp.concatenate([s, s], 1)

    for m in range(n // 256):
        rows = slice(m * 256, m * 256 + 256)
        raw = dot(x_s[rows, :], w_ref[...])
        c, s = both(rows)
        q_s[rows, :] = (turn(raw[:, 0:lanes], c, s, 1.0) * scaling).astype(BF16)
        keys = turn(raw[:, lanes:2 * lanes], c, s, 1.0).astype(BF16)
        k_s[rows, :] = keys
        kt_s[:, rows] = keys.T
        vals = raw[:, 2 * lanes:].astype(BF16)
        v_s[rows, :] = vals
        vt_s[:, rows] = vals.T
        do_s[rows, :] = dot_nt(g_ref[rows, :], wo1_ref[...]).astype(BF16)

    tick(1)
    tile = TILE
    lane = lax.broadcasted_iota(jnp.int32, (tile, 128), 1)
    work = [(h, i) for i in reversed(range(n // tile)) for h in range(4)]

    def first(h, i):
        span = (i + 1) * tile
        here = slice(i * tile, span)
        cols = slice(h // 2 * 128, h // 2 * 128 + 128)
        mine = (lane < HEAD_DIM) if h % 2 == 0 else (lane >= HEAD_DIM)
        qh = jnp.where(mine, q_s[here, cols], 0).astype(BF16)
        doh = jnp.where(mine, do_s[here, cols], 0).astype(BF16)
        return qh, doh, dot_nt(k_s[0:span, cols], qh), dot_nt(v_s[0:span, cols], doh)

    def second(h, i, qh, doh, st, dpt):
        span = (i + 1) * tile
        here = slice(i * tile, span)
        cols = slice(h // 2 * 128, h // 2 * 128 + 128)
        rows = slice(h * HEAD_DIM, (h + 1) * HEAD_DIM)
        family = famc_s[0:span, :]
        allowed = jnp.concatenate([family] * (tile // 128), 1) == famr_s[:, here]
        key_place = lax.broadcasted_iota(jnp.int32, (span, tile), 0)
        query_place = lax.broadcasted_iota(jnp.int32, (span, tile), 1) + i * tile
        st = jnp.where(allowed & (key_place <= query_place), st, -1e9)
        e = jnp.exp(st - jnp.max(st, 0, keepdims=True))
        p = e * (1.0 / jnp.sum(e, 0, keepdims=True))
        pb = p.astype(BF16)
        ds = (p * (dpt - jnp.sum(p * dpt, 0, keepdims=True))).astype(BF16)
        ht_s[rows, here] = dot(vt_s[rows, 0:span], pb).astype(BF16)
        dqt_s[rows, here] = dot(kt_s[rows, 0:span], ds) * scaling
        dv = dot(pb, doh)
        dk = dot(ds, qh)
        if h % 2 == 0 and i == n // tile - 1:
            dv_s[:, cols] = dv
            dk_s[:, cols] = dk
        else:
            dv_s[0:span, cols] += dv
            dk_s[0:span, cols] += dk

    made_first = first(*work[0])
    for j, (h, i) in enumerate(work):
        later = first(*work[j + 1]) if j + 1 < len(work) else None
        second(h, i, *made_first)
        made_first = later
        if h == 3 and i != 1:
            tick({3: 2, 2: 3, 0: 4}[i])

    @pl.when(step > 0)
    def _():
        if linked:
            sent, mine = heads_out(step - 1)
            for copy in sent:
                copy.wait_send()
            mine.wait()
        else:
            local_copy(heads_s, heads_ref.at[:, pl.ds(pl.multiple_of((step - 1) * lanes, lanes), lanes)], h_sem.at[0]).wait()
    heads_s[...] = ht_s[...].T
    if linked:
        sent, mine = heads_out(step)
        for copy in sent:
            copy.start()
        mine.start()
    else:
        local_copy(heads_s, heads_ref.at[:, pl.ds(pl.multiple_of(step * lanes, lanes), lanes)], h_sem.at[0]).start()

    @functools.partial(each_band, n // 256)
    def _(rows, m):
        c, s = both(rows)
        draw_s[rows, 0:lanes] = turn(dqt_s[:, rows].T, c, s, -1.0).astype(BF16)
        draw_s[rows, lanes:2 * lanes] = turn(dk_s[rows, :], c, s, -1.0).astype(BF16)
        draw_s[rows, 2 * lanes:] = dv_s[rows, :].astype(BF16)

    for m in range(d // 256):
        grads = dot(xt_s[m * 256:(m + 1) * 256, :], draw_s[...]).astype(BF16)
        gq_s[m, 0] = grads[0:128]
        gq_s[m, 1] = grads[128:256]
    go_s[...] = dot(ht_s[...], g_ref[...]).astype(BF16)
    for copy in results(step):
        copy.start()
    tick(5)
    for m in range(n // 256):
        here = slice(m * 256, (m + 1) * 256)
        dn = dot_nt(draw_s[here, :], w_ref[...])

        @pl.when(step == 0)
        def _():
            dn_s[here, :] = dn

        @pl.when(step > 0)
        def _():
            dn_s[here, :] += dn

    @pl.when(step == last)
    def _():
        sums_ref[...] = jnp.zeros_like(sums_ref)

        @functools.partial(each_band, n // 256)
        def _(here, m):
            total = dn_s[here, :]
            xhat, _ = normalize(raw_ref[here, :].astype(F32))
            sums_ref[0:1, :] += jnp.sum(total * xhat, 0, keepdims=True)
            sums_ref[1:2, :] += jnp.sum(total, 0, keepdims=True)
            dn_ref[here, :] = total.astype(BF16)

    tick(6)

    @pl.when(step == last)
    def _():
        for copy in results(step):
            copy.wait()
        if linked:
            for at in range(steps):
                for copy in heads_out(at)[0]:
                    copy.wait_recv()
            for copy in heads_out(step)[0]:
                copy.wait_send()
            heads_out(step)[1].wait()
        else:
            local_copy(heads_s, heads_ref.at[:, pl.ds(pl.multiple_of(step * lanes, lanes), lanes)], h_sem.at[0]).wait()


def attend(raw, g, gain, shift, wqkv, wo, families, linked, grads=None):
    n, d = raw.shape
    pair_lane = np.arange(128) % HEAD_DIM % (ROT // 2)
    freq = 10000.0 ** (-2.0 * pair_lane / ROT)
    high, low = np.arange(n // 32)[:, None] * 32.0 * freq, np.arange(32)[:, None] * freq
    tab = jnp.asarray(np.stack([np.cos(high), np.sin(high), np.cos(low), np.sin(low)]), F32)
    sd, vm = jax.ShapeDtypeStruct, pltpu.VMEM
    out_shape = [sd((n, d), BF16), sd((8, d), F32), sd((2, 4, 2, 128, 3 * d // 2) if linked else (4, 2, 128, 3 * d), BF16),
                 sd((4, 2, 128, d), BF16), sd((4, n // 4, d) if linked else (n, d), BF16)]
    out_specs = [whole((n, d)), whole((8, d))] + [ANYWHERE] * 3
    scratch = [vm((n, d), BF16), vm((d, n), BF16), vm((n, 128), F32), vm((n, 128), F32), vm((2, d, 768), BF16), vm((2, 256, d), BF16)]
    scratch += [vm((n, 256), BF16)] * 4 + [vm((256, n), BF16)] * 3
    scratch += [vm((256, n), F32), vm((n, 256), F32), vm((n, 256), F32), vm((n, 768), BF16), vm((n, d), F32), vm((4, 2, 128, 768), BF16),
                vm((256, d), BF16), vm((n, 256), BF16), vm((1, n), F32), vm((n, 128), F32), DMA((2, 6)), DMA((2, 2)), DMA((6,)), DMA((2,)), DMA((1,))]
    params, more = {}, []
    if linked:
        more = [grads]
        out_shape += [sd((128, 256), F32)] * 4 + [sd((128, 384), F32)]
        out_specs += [whole((128, 256))] * 4 + [whole((128, 384))]
        scratch += [DMA((4, 3)), DMA((4, 3))]
        scratch += piece_scratch(256, AT_SPLIT) * 2 + piece_scratch(384, EARLY_SPLIT)
        params = dict(collective_id=1, has_side_effects=True)
    return pl.pallas_call(
        functools.partial(attn_kernel, linked=linked), out_shape=out_shape, grid=(len(ORDER),),
        in_specs=[whole((n, d)), whole((n, d)), whole((1, d)), whole((1, d)), whole(families.shape), whole((4, 32, 128)), ANYWHERE, ANYWHERE]
        + [ANYWHERE] * len(more),
        out_specs=out_specs, scratch_shapes=scratch,
        compiler_params=pltpu.CompilerParams(vmem_limit_bytes=60 * 2**20, **params),
        cost_estimate=pl.CostEstimate(flops=70_000_000_000, bytes_accessed=30_000_000, transcendentals=20_000_000),
    )(raw, g, gain.reshape(1, d), shift.reshape(1, d), families, tab, wqkv, wo, *more)


class SmallSum:
    def __init__(self, place, held, heard, by_z, send, recv):
        self.p, self.held, self.heard, self.by_z, self.send, self.recv = place, held, heard, by_z, send, recv

    def copies(self, t):
        p = self.p
        if t < 3:
            to = (p.twin, p.beside_y, p.beside_x)[t]
            return [remote_copy(self.held, self.heard.at[t], self.send.at[t], self.recv.at[t], to)]
        return [remote_copy(self.by_z.at[p.z], self.by_z.at[p.z], self.send.at[3 + j], self.recv.at[3 + j], to)
                for j, to in enumerate(p.along_z)]

    def tick(self, t):
        if t > 0:
            for copy in self.copies(t - 1):
                copy.wait()
        if 0 < t < 4:
            total = self.held[...] + self.heard[t - 1]
            if t < 3:
                self.held[...] = total
            else:
                self.by_z[self.p.z] = total
        if t < 4:
            for copy in self.copies(t):
                copy.start()
        return None if t < 4 else self.by_z[0] + self.by_z[1] + self.by_z[2] + self.by_z[3]


def tail_kernel(dat_ref, heads_ref, gq_ref, go_ref, inp_ref, g_ref, y_ref, dn_ref, wo_ref, gain_ref, dbias_ref, sums_ff_ref, sums_at_ref,
                ub_ref, early_ref, lo_ref, ig_ref, qkv_ref, out_ref, gain_o, shift_o, ub_o, db_o,
                back_s, inp_s, g_s, heads_s, y_s, dn_s, wo_s, lo_s, ig_s, small_s, heard_s, by_z_s,
                load_sem, wo_sem, back_send, back_recv, own_sem, small_send, small_recv, lo_sem, ig_sem, *pieces):
    place = Place()
    d = wo_s.shape[0]
    place.greet()
    swaps = [remote_copy(dat_ref.at[to], back_s.at[place.seq], back_send.at[j], back_recv.at[j], device)
             for j, (to, device) in enumerate(place.peers)]
    own = local_copy(dat_ref.at[place.seq], back_s.at[place.seq], own_sem.at[0])
    blocks = {}

    def part(source, w, row0, rows):
        return lambda y, c: source.at[:, :, pl.ds(row0, rows), pl.ds(pl.multiple_of((y * 2 + c) * w, 128), w)]

    def out_done(total):
        out_ref[...] = total

    def qkv_done(row0):
        def done(total):
            rows = slice(row0, row0 + total.shape[0])
            early = early_ref[rows, :]
            first = jnp.where(place.c == 0, early, total)
            second = jnp.where(place.c == 0, total, early)
            order = ((first, 0), (second, 0), (second, 1), (first, 1), (first, 2), (second, 2))
            for k, (source, at) in enumerate(order):
                qkv_ref[rows, k * 128:(k + 1) * 128] = source[:, at * 128:(at + 1) * 128]
        return done

    cuts = [0, piece_count(TAIL_SPLITS[0])]
    for split in TAIL_SPLITS[1:]:
        cuts.append(cuts[-1] + piece_count(split))
    late = gq_ref.at[1]
    row1 = sum(TAIL_SPLITS[1])
    made = [Piece(place, part(go_ref, 256, 0, 128), out_done, TAIL_SPLITS[0], pieces[:cuts[1]]),
            Piece(place, part(late, 384, 0, row1), qkv_done(0), TAIL_SPLITS[1], pieces[cuts[1]:cuts[2]]),
            Piece(place, part(late, 384, row1, 128 - row1), qkv_done(row1), TAIL_SPLITS[2], pieces[cuts[2]:])]
    small = SmallSum(place, small_s, heard_s, by_z_s, small_send, small_recv)
    small_s[0:3, :] = sums_ff_ref[0:3, :]
    small_s[0:2, :] += sums_at_ref[0:2, :]
    small_s[3:4, :] = jnp.zeros((1, d), F32)
    for k in range(4):
        small_s[4 + k:5 + k, :] = ub_ref[:, k * d:(k + 1) * d]
    for piece in made:
        piece.tick(0)
    for copy in swaps:
        copy.start()
    small.tick(0)
    loads = [local_copy(a, b, load_sem.at[k]) for k, (a, b) in enumerate(
        ((heads_ref, heads_s), (inp_ref, inp_s), (y_ref, y_s), (g_ref, g_s), (dn_ref, dn_s)))]
    for pair in range(d // 128):
        at = [p for two in ORDER for p in two].index(pair)
        blocks[at] = local_copy(wo_ref.at[pl.ds(pair * 128, 128), :], wo_s.at[pl.ds(at * 128, 128), :], wo_sem.at[at])
    for copy in [loads[0]] + list(blocks.values()) + loads[1:] + [own]:
        copy.start()

    def lo_out(r):
        return local_copy(lo_s.at[r], lo_ref.at[r], lo_sem.at[r])

    def ig_out(r):
        return local_copy(ig_s.at[r], ig_ref.at[r], ig_sem.at[r])

    def forward(r):
        total = inp_s[r].astype(F32) + dot(heads_s[r], wo_s[...]) + (y_s[r] + dbias_ref[...])
        lo_s[r] = total.astype(BF16)
        lo_out(r).start()

    def backward(r):
        xhat, scale = normalize(inp_s[r].astype(F32))
        dx = (dn_s[r] + back_s[r].astype(F32)) * gain_ref[...]
        ig_s[r] = g_s[r].astype(F32) + (dx - jnp.mean(dx, -1, keepdims=True) - xhat * jnp.mean(dx * xhat, -1, keepdims=True)) * scale
        ig_out(r).start()

    made[0].tick(1)
    small.tick(1)
    for copy in list(blocks.values()) + loads[:3]:
        copy.wait()
    forward(0)
    forward(1)
    made[1].tick(1)
    forward(2)
    forward(3)
    made[0].tick(2)
    made[2].tick(1)
    small.tick(2)
    loads[3].wait()
    loads[4].wait()
    own.wait()
    backward(place.seq)
    made[1].tick(2)
    made[0].tick(3)
    small.tick(3)
    for j in range(3):
        swaps[j].wait_send()
    swaps[2].wait_recv()
    backward((place.seq + 1) % 4)
    made[2].tick(2)
    made[1].tick(3)
    swaps[1].wait_recv()
    backward((place.seq + 2) % 4)
    made[2].tick(3)
    swaps[0].wait_recv()
    backward((place.seq + 3) % 4)
    total = small.tick(4)
    for piece in made:
        piece.tick(4)
    gain_o[...] = total[0:1]
    shift_o[...] = total[1:2]
    db_o[...] = total[2:3]
    for k in range(4):
        ub_o[:, k * d:(k + 1) * d] = total[4 + k:5 + k]
    for r in range(4):
        lo_out(r).wait()
        ig_out(r).wait()


def finish(dat, heads, gq, go, inp, g, y, dn, wo, gain, dbias, sums_ff, sums_at, ub, early):
    sd, vm = jax.ShapeDtypeStruct, pltpu.VMEM
    shape, d = inp.shape, inp.shape[2]
    vmem = pl.BlockSpec(memory_space=pltpu.VMEM)
    return pl.pallas_call(
        tail_kernel,
        out_shape=[sd(shape, BF16), sd(shape, F32), sd((128, 768), F32), sd((128, 256), F32), sd((1, d), F32), sd((1, d), F32), sd((1, 4 * d), F32),
                   sd((1, d), F32)],
        in_specs=[ANYWHERE] * 9 + [vmem] * 6, out_specs=[ANYWHERE] * 2 + [vmem] * 6,
        scratch_shapes=[vm(shape, BF16)] * 4 + [vm(shape, F32)] * 2 + [vm((d, d), BF16), vm(shape, BF16), vm(shape, F32),
                        vm((8, d), F32), vm((3, 8, d), F32), vm((4, 8, d), F32),
                        DMA((5,)), DMA((8,)), DMA((3,)), DMA((3,)), DMA((1,)), DMA((6,)), DMA((6,)), DMA((4,)), DMA((4,))]
        + piece_scratch(256, TAIL_SPLITS[0]) + piece_scratch(384, TAIL_SPLITS[1]) + piece_scratch(384, TAIL_SPLITS[2]),
        compiler_params=pltpu.CompilerParams(collective_id=2, has_side_effects=True, vmem_limit_bytes=56 * 2**20),
    )(dat.reshape(shape), heads, gq, go, inp, g, y.reshape(shape), dn.reshape(shape), wo, gain.reshape(1, d), dbias.reshape(1, d), sums_ff, sums_at,
      ub, early)


def on_device(inputs, norm_gain, norm_shift, qkv_weight, out_weight, up_weight, up_bias, down_weight, down_bias, partners, families, cotangent, linked):
    row_count, place_count, width = inputs.shape
    tokens = row_count * place_count
    local_rows = partners - lax.axis_index("dp") * row_count
    grad = jnp.take(cotangent, local_rows, axis=0, mode="clip")
    branch_args = norm_gain, norm_shift, qkv_weight, out_weight, families, linked
    if linked:
        y, dn, sums_ff, ub, grads, row_inputs, row_grad, up0, down0, up1, down1 = feed_forward(inputs, grad, norm_gain, norm_shift, up_bias, up_weight, down_weight, True)
        dat, sums_at, gq, go, heads, up2, down2, up3, down3, early = attend(
            row_inputs.reshape(tokens, width), row_grad.reshape(tokens, width), *branch_args, grads)
        layer_out, input_grad, qkv_sum, out_sum, gain_sum, shift_sum, ub_sum, db_sum = finish(
            dat, heads, gq, go, inputs, grad, y, dn, out_weight, norm_gain, down_bias, sums_ff, sums_at, ub, early)
        ups = (up0, up1, up2, up3)
        up_sum = jnp.concatenate([u[:, :128] for u in ups] + [u[:, 128:] for u in ups], 1)
        down_sum = jnp.concatenate([down0, down1, down2, down3], 0)
        return (layer_out, input_grad, gain_sum.reshape(width), shift_sum.reshape(width), qkv_sum, out_sum, up_sum, ub_sum.reshape(-1), down_sum,
                db_sum.reshape(width))
    swap = functools.partial(lax.all_to_all, axis_name="seq", split_axis=0, concat_axis=0, tiled=True)
    row_inputs, row_grad = swap(inputs).reshape(tokens, width), swap(grad).reshape(tokens, width)
    y, dn, sums_ff, ub, up_grad, down_grad = feed_forward(inputs, grad, norm_gain, norm_shift, up_bias, up_weight, down_weight, False)
    dat, sums_at, qkv_grad, out_grad, heads = attend(row_inputs, row_grad, *branch_args)

    def scatter(parts, columns):
        part = lax.psum_scatter(parts.reshape(-1, columns), "seq", scatter_dimension=1, tiled=True)
        return lax.psum_scatter(part, "dp", scatter_dimension=0, tiled=True).astype(F32)

    qkv_sum, out_sum = scatter(qkv_grad, 3 * width), scatter(out_grad, width)
    up_sum, down_sum = scatter(up_grad, up_bias.shape[0]), scatter(down_grad, width)
    heads = swap(heads.reshape(inputs.shape)).reshape(tokens, width)
    order = np.array([p for two in ORDER for p in two])
    attn_out = dot(heads, out_weight.reshape(-1, 128, width)[order].reshape(width, width))
    values = inputs.astype(F32).reshape(tokens, width)
    layer_out = (values + attn_out + (y + down_bias)).astype(BF16).reshape(inputs.shape)
    xhat, scale = normalize(values)
    dx = (dn + swap(dat.reshape(inputs.shape)).reshape(tokens, width).astype(F32)) * norm_gain
    input_grad = grad.reshape(tokens, width).astype(F32) + (dx - jnp.mean(dx, -1, keepdims=True) - xhat * jnp.mean(dx * xhat, -1, keepdims=True)) * scale
    gain_sum, shift_sum, up_bias_sum, down_bias_sum = lax.psum((sums_ff[0] + sums_at[0], sums_ff[1] + sums_at[1], ub[0], sums_ff[2]), ("dp", "seq"))
    return (layer_out, input_grad.reshape(inputs.shape), gain_sum, shift_sum, qkv_sum, out_sum, up_sum, up_bias_sum, down_sum, down_bias_sum)


def solution(mesh):
    rows = P("dp", "seq", None)
    placed = (rows,) + (P(),) * 8 + (P("dp"), P("dp", None), rows)
    grads = P("dp", "seq")
    linked = (mesh.shape["dp"], mesh.shape["seq"]) == (8, 4)
    return jax.shard_map(functools.partial(on_device, linked=linked), mesh=mesh, in_specs=placed,
                         out_specs=(rows, rows, P(), P(), grads, grads, grads, P(), grads, P()), check_vma=False)
```

profile of v0, /device:TPU:0, one launch (start us, length us, event | category | flops | bytes accessed | tf_op | source)
XLA Modules:
  0.0 251.2 jit_solution(8316591403273287714)
XLA Ops:
  0.6 0.0 copy-start
  0.7 0.8 broadcast_subtract_fusion
  1.5 0.8 copy-done
  2.3 2.0 gather_fusion
  4.3 93.3 %shard_map.204 = (f32[1024,1024]{1,0:T(8,128)}, f32[1024,1024]{1,0:T(8,128)}, f32[8,1024]{1,0:T(8,128)}, f32[1,4096]{1,0:T(1,128)}, bf16[4,4,2,256,1024]{4,3,2,1...) custom-call(bf16[1024,1024]{1,0:T(8,128)(2,1)} %bitcast.18, ...), custom_call_target="tpu_custom_call" | custom-call | flops 51999997952 | bytes 50000000 | tf_op jit(solution)/shard_map/pallas_call | solution.py:401
  97.6 96.6 %shard_map.205 = (bf16[1024,1024]{1,0:T(8,128)(2,1)}, f32[8,1024]{1,0:T(8,128)}, bf16[2,4,2,128,1536]{4,3,2,1,0:T(8,128)(2,1)}, bf16[4,2,128,1024]{3,2,1,0:T(8,1...) custom-call(bf16[1024,1024]{1,0:T(8,128)(2,1)} %bitcast.31, ...), custom_call_target="tpu_custom_call" | custom-call | flops 70000001024 | bytes 30000000 | tf_op jit(solution)/shard_map/pallas_call | solution.py:719
  194.2 0.0 copy-start.10
  194.2 0.0 copy-start.11
  194.2 0.0 copy-start.12
  194.2 0.0 copy-start.13
  194.2 0.0 copy-start.6
  194.2 0.0 copy-start.5
  194.2 0.0 copy-start.9
  194.2 0.0 copy-start.8
  194.2 46.0 %shard_map.206 = (bf16[4,256,1024]{2,1,0:T(8,128)(2,1)}, f32[4,256,1024]{2,1,0:T(8,128)}, f32[128,768]{1,0:T(8,128)}, f32[128,256]{1,0:T(8,128)}, f32[1,1024]{1,...) custom-call(bf16[4,256,1024]{2,1,0:T(8,128)(2,1)} %bitcast.19, ...), custom_call_target="tpu_custom_call" | custom-call | tf_op jit(solution)/shard_map/pallas_call | solution.py:877
  240.3 0.0 copy-start.3
  240.3 0.0 copy-done.10
  240.3 0.0 copy-done.11
  240.3 0.0 copy-done.12
  240.3 0.0 copy-done.13
  240.3 0.8 pad_maximum_fusion
  241.2 0.0 copy-done.6
  241.2 0.0 copy-done.5
  241.2 0.0 copy-done.9
  241.2 0.0 copy-done.8
  241.3 0.8 copy-done.3
  242.1 0.0 copy-start.15
  242.1 0.0 copy-start.2
  242.1 1.3 copy.38
  243.4 0.2 copy-done.15
  243.5 1.7 copy-done.2
  245.2 0.0 copy-start.18
  245.2 0.0 copy-start.17
  245.2 0.0 copy-start.4
  245.2 0.0 copy-start.7
  245.2 0.0 copy-start.14
  245.2 0.0 copy-start.16
  245.2 0.0 copy-start.1
  245.2 2.1 copy.39
  247.4 0.0 copy-done.18
  247.4 0.6 copy.40
  248.0 0.0 copy-done.17
  248.0 0.6 copy.41
  248.6 0.0 copy-done.4
  248.6 0.7 copy.42
  249.3 0.0 copy-done.7
  249.3 0.7 copy.43
  250.0 0.0 copy-done.14
  250.0 0.6 copy.44
  250.6 0.0 copy-done.16
  250.6 0.6 copy.45
  251.2 0.0 copy-done.1
  (9 shorter events, 0.1 us)
Async XLA Ops:
  0.6 1.6 copy-start
  194.2 46.1 %copy-start.10 = (f32[128,256]{1,0:T(8,128)S(1)}, f32[128,256]{1,0:T(8,128)}, u32[]{:S(2)}) copy-start(f32[128,256]{1,0:T(8,128)} %get-tuple-element.63) | copy-start | bytes 393220
  194.2 46.1 %copy-start.11 = (f32[128,256]{1,0:T(8,128)S(1)}, f32[128,256]{1,0:T(8,128)}, u32[]{:S(2)}) copy-start(f32[128,256]{1,0:T(8,128)} %get-tuple-element.64) | copy-start | bytes 393220
  194.2 46.1 %copy-start.12 = (f32[128,256]{1,0:T(8,128)S(1)}, f32[128,256]{1,0:T(8,128)}, u32[]{:S(2)}) copy-start(f32[128,256]{1,0:T(8,128)} %get-tuple-element.65) | copy-start | bytes 393220
  194.2 46.1 %copy-start.13 = (f32[128,256]{1,0:T(8,128)S(1)}, f32[128,256]{1,0:T(8,128)}, u32[]{:S(2)}) copy-start(f32[128,256]{1,0:T(8,128)} %get-tuple-element.66) | copy-start | bytes 393220
  194.2 47.0 %copy-start.6 = (f32[128,256]{1,0:T(8,128)S(1)}, f32[128,256]{1,0:T(8,128)}, u32[]{:S(2)}) copy-start(f32[128,256]{1,0:T(8,128)} %get-tuple-element.58) | copy-start | bytes 393220
  194.2 47.0 %copy-start.5 = (f32[128,256]{1,0:T(8,128)S(1)}, f32[128,256]{1,0:T(8,128)}, u32[]{:S(2)}) copy-start(f32[128,256]{1,0:T(8,128)} %get-tuple-element.59) | copy-start | bytes 393220
  194.2 47.0 %copy-start.9 = (f32[128,256]{1,0:T(8,128)S(1)}, f32[128,256]{1,0:T(8,128)}, u32[]{:S(2)}) copy-start(f32[128,256]{1,0:T(8,128)} %get-tuple-element.60) | copy-start | bytes 393220
  194.2 47.0 %copy-start.8 = (f32[128,256]{1,0:T(8,128)S(1)}, f32[128,256]{1,0:T(8,128)}, u32[]{:S(2)}) copy-start(f32[128,256]{1,0:T(8,128)} %get-tuple-element.61) | copy-start | bytes 393220
  240.3 1.8 copy-start.3
  242.1 1.5 copy-start.15
  242.1 3.1 %copy-start.2 = (f32[4,256,1024]{2,1,0:T(8,128)S(1)}, f32[4,256,1024]{2,1,0:T(8,128)}, u32[]{:S(2)}) copy-start(f32[4,256,1024]{2,1,0:T(8,128)} %get-tuple-element.79) | copy-start | bytes 12582916
  245.2 2.2 copy-start.18
  245.2 2.8 %copy-start.17 = (f32[1,1024]{1,0:T(1,128)S(1)}, f32[1,1024]{1,0:T(1,128)}, u32[]{:S(2)}) copy-start(f32[1,1024]{1,0:T(1,128)} %get-tuple-element.55) | copy-start | bytes 12292
  245.2 3.4 %copy-start.4 = (f32[128,768]{1,0:T(8,128)S(1)}, f32[128,768]{1,0:T(8,128)}, u32[]{:S(2)}) copy-start(f32[128,768]{1,0:T(8,128)} %get-tuple-element.82) | copy-start | bytes 1179652
  245.2 4.1 %copy-start.7 = (f32[128,256]{1,0:T(8,128)S(1)}, f32[128,256]{1,0:T(8,128)}, u32[]{:S(2)}) copy-start(f32[128,256]{1,0:T(8,128)} %get-tuple-element.83) | copy-start | bytes 393220
  245.2 4.8 %copy-start.14 = (f32[1,4096]{1,0:T(1,128)S(1)}, f32[1,4096]{1,0:T(1,128)}, u32[]{:S(2)}) copy-start(f32[1,4096]{1,0:T(1,128)} %get-tuple-element.62) | copy-start | bytes 49156
  245.2 5.4 %copy-start.16 = (f32[1,1024]{1,0:T(1,128)S(1)}, f32[1,1024]{1,0:T(1,128)}, u32[]{:S(2)}) copy-start(f32[1,1024]{1,0:T(1,128)} %get-tuple-element.67) | copy-start | bytes 12292
  245.2 6.0 %copy-start.1 = (bf16[4,256,1024]{2,1,0:T(8,128)(2,1)S(1)}, bf16[4,256,1024]{2,1,0:T(8,128)(2,1)}, u32[]{:S(2)}) copy-start(bf16[4,256,1024]{2,1,0:T(8,128)(2,1)} %param.24) | copy-start | bytes 6291460
where the time goes:
time: 251 us
  Pallas kernels  236 us (94%)
  local copies, waits for them, and re-layouts  12.7 us (5%)
    pallas_call x1, Pallas kernels, attend(): pl.pallas_call(functools.partial(attn_kernel, linked=linked), out_shape=o...  96.6 us
    pallas_call x1, Pallas kernels, feed_forward(): pl.pallas_call(functools.partial(ff_kernel, linked=linked), out_shape=out...  93.3 us
    pallas_call x1, Pallas kernels, finish(): pl.pallas_call(tail_kernel, out_shape=[sd(shape, BF16), sd(shape, F32), s...  46 us
    unnamed x53, local copies, waits for them, and re-layouts  10.7 us

commit v1 on v0

--- a/solution.py
+++ b/solution.py
@@ -217,12 +217,12 @@
             self.done(jnp.concatenate(parts, 0) if len(parts) > 1 else parts[0])
 
 
-def ff_kernel(inp_ref, g_ref, gain_ref, shift_ref, bias_ref, wu_ref, wd_ref, *rest, linked):
-    hand, rest = (rest[:2], rest[2:]) if linked else ((), rest)
+def ff_kernel(part_ref, inp_ref, cot_ref, gain_ref, shift_ref, bias_ref, wu_ref, wd_ref, *rest, linked):
+    hand, rest = (rest[:1], rest[1:]) if linked else ((), rest)
     y_ref, dn_ref, sums_ref, ub_ref = rest[:4]
     outs, rest = (rest[4:11], rest[11:]) if linked else (rest[4:6], rest[6:])
-    x_s, xt_s, act_s, dh_s, wu_s, wd_s, gu_s, gd_s, wu_sem, wd_sem, gu_sem, gd_sem = rest[:12]
-    rest = rest[12:]
+    x_s, xt_s, act_s, dh_s, wu_s, wd_s, gu_s, gd_s, g_ref, wu_sem, wd_sem, gu_sem, gd_sem = rest[:13]
+    rest = rest[13:]
     step = pl.program_id(0)
     last = pl.num_programs(0) - 1
     n, d = x_s.shape
@@ -263,13 +263,15 @@
         row_send, row_recv, own_sem = rest[:3]
         rest = rest[3:]
 
-        def swaps():
-            out = []
-            for a in range(2):
-                for j, (to, device) in enumerate(place.peers):
-                    out.append(remote_copy(hand[a].at[to], outs[1 + a].at[place.seq], row_send.at[a, j], row_recv.at[a, j], device))
-                out.append(local_copy(hand[a].at[place.seq], outs[1 + a].at[place.seq], own_sem.at[a]))
-            return out
+        def swaps(a):
+            span = n // 4
+
+            def row(at):
+                return g_ref.at[pl.ds(pl.multiple_of(at * span, span), span), :] if a else hand[0].at[at]
+
+            out = [remote_copy(row(to), outs[1 + a].at[place.seq], row_send.at[a, j], row_recv.at[a, j], device)
+                   for j, (to, device) in enumerate(place.peers)]
+            return out + [local_copy(row(place.seq), outs[1 + a].at[place.seq], own_sem.at[a])]
 
         def part_of(k):
             return lambda y, c: outs[0].at[k, :, :, :, pl.ds(pl.multiple_of((y * 2 + c) * 256, 256), 256)]
@@ -295,7 +297,13 @@
             copy.start()
         if linked:
             place.greet()
-            for copy in swaps():
+            for copy in swaps(0):
+                copy.start()
+        count, span, _ = cot_ref.shape
+        for r in range(count):
+            g_ref[r * span:(r + 1) * span, :] = cot_ref[lax.rem(part_ref[r], count)]
+        if linked:
+            for copy in swaps(1):
                 copy.start()
         sums_ref[...] = jnp.zeros_like(sums_ref)
 
@@ -376,21 +384,21 @@
         for copy in results(step):
             copy.wait()
         if linked:
-            for copy in swaps():
+            for copy in swaps(0) + swaps(1):
                 copy.wait()
 
 
-def feed_forward(inp, g, gain, shift, bias, wu, wd, linked):
+def feed_forward(inp, cot, partners, gain, shift, bias, wu, wd, linked):
     rows, span, d = inp.shape
     n, hidden = rows * span, bias.shape[0]
     sd, vm = jax.ShapeDtypeStruct, pltpu.VMEM
     out_shape = [sd((n, d), F32), sd((n, d), F32), sd((8, d), F32), sd((1, hidden), F32)]
     out_specs = [whole((n, d)), whole((n, d)), whole((8, d)), whole((1, hidden))]
     scratch = [vm((n, d), BF16), vm((d, n), BF16), vm((n, 512), BF16), vm((n, 512), BF16), vm((2, d, 512), BF16), vm((2, 512, d), BF16),
-               vm((4, 2, 128, 512), BF16), vm((512, d), BF16), DMA((2, 4)), DMA((2, 4)), DMA((4,)), DMA((4,))]
+               vm((4, 2, 128, 512), BF16), vm((512, d), BF16), vm((n, d), BF16), DMA((2, 4)), DMA((2, 4)), DMA((4,)), DMA((4,))]
     more, params = [], {}
     if linked:
-        more = [inp, g]
+        more = [inp]
         out_shape += [sd((4, 4, 2, 256, d), BF16), sd(inp.shape, BF16), sd(inp.shape, BF16), *[sd((128, 256), F32)] * 4]
         out_specs += [ANYWHERE] * 3 + [whole((128, 256))] * 4
         scratch += [DMA((2, 3)), DMA((2, 3)), DMA((2,))] + piece_scratch(256, FF_SPLITS[0]) + piece_scratch(256, FF_SPLITS[1])
@@ -400,11 +408,11 @@
         out_specs += [ANYWHERE] * 2
     return pl.pallas_call(
         functools.partial(ff_kernel, linked=linked), out_shape=out_shape, grid=(hidden // 512,),
-        in_specs=[whole((n, d)), whole((n, d)), whole((1, d)), whole((1, d)), whole((1, hidden)), ANYWHERE, ANYWHERE] + [ANYWHERE] * len(more),
+        in_specs=[pl.BlockSpec(memory_space=pltpu.SMEM), whole((n, d)), whole(cot.shape), whole((1, d)), whole((1, d)), whole((1, hidden)), ANYWHERE, ANYWHERE] + [ANYWHERE] * len(more),
         out_specs=out_specs, scratch_shapes=scratch,
         compiler_params=pltpu.CompilerParams(vmem_limit_bytes=58 * 2**20, **params),
         cost_estimate=pl.CostEstimate(flops=52_000_000_000, bytes_accessed=50_000_000, transcendentals=4_000_000),
-    )(inp.reshape(n, d), g.reshape(n, d), gain.reshape(1, d), shift.reshape(1, d), bias.reshape(1, hidden), wu, wd, *more)
+    )(partners, inp.reshape(n, d), cot, gain.reshape(1, d), shift.reshape(1, d), bias.reshape(1, hidden), wu, wd, *more)
 
 
 def turn(x, c, s, sign):
@@ -638,8 +646,8 @@
     else:
         local_copy(heads_s, heads_ref.at[:, pl.ds(pl.multiple_of(step * lanes, lanes), lanes)], h_sem.at[0]).start()
 
-    @functools.partial(each_band, n // 256)
-    def _(rows, m):
+    for m in range(n // 256):
+        rows = slice(m * 256, m * 256 + 256)
         c, s = both(rows)
         draw_s[rows, 0:lanes] = turn(dqt_s[:, rows].T, c, s, -1.0).astype(BF16)
         draw_s[rows, lanes:2 * lanes] = turn(dk_s[rows, :], c, s, -1.0).astype(BF16)
@@ -754,7 +762,7 @@
         return None if t < 4 else self.by_z[0] + self.by_z[1] + self.by_z[2] + self.by_z[3]
 
 
-def tail_kernel(dat_ref, heads_ref, gq_ref, go_ref, inp_ref, g_ref, y_ref, dn_ref, wo_ref, gain_ref, dbias_ref, sums_ff_ref, sums_at_ref,
+def tail_kernel(dat_ref, heads_ref, gq_ref, go_ref, inp_ref, cot_ref, y_ref, dn_ref, wo_ref, part_ref, gain_ref, dbias_ref, sums_ff_ref, sums_at_ref,
                 ub_ref, early_ref, lo_ref, ig_ref, qkv_ref, out_ref, gain_o, shift_o, ub_o, db_o,
                 back_s, inp_s, g_s, heads_s, y_s, dn_s, wo_s, lo_s, ig_s, small_s, heard_s, by_z_s,
                 load_sem, wo_sem, back_send, back_recv, own_sem, small_send, small_recv, lo_sem, ig_sem, *pieces):
@@ -803,7 +811,7 @@
         copy.start()
     small.tick(0)
     loads = [local_copy(a, b, load_sem.at[k]) for k, (a, b) in enumerate(
-        ((heads_ref, heads_s), (inp_ref, inp_s), (y_ref, y_s), (g_ref, g_s), (dn_ref, dn_s)))]
+        ((heads_ref, heads_s), (inp_ref, inp_s), (y_ref, y_s), (cot_ref, g_s), (dn_ref, dn_s)))]
     for pair in range(d // 128):
         at = [p for two in ORDER for p in two].index(pair)
         blocks[at] = local_copy(wo_ref.at[pl.ds(pair * 128, 128), :], wo_s.at[pl.ds(at * 128, 128), :], wo_sem.at[at])
@@ -816,26 +824,25 @@
     def ig_out(r):
         return local_copy(ig_s.at[r], ig_ref.at[r], ig_sem.at[r])
 
-    def forward(r):
+    def forward(r, carry):
         total = inp_s[r].astype(F32) + dot(heads_s[r], wo_s[...]) + (y_s[r] + dbias_ref[...])
         lo_s[r] = total.astype(BF16)
         lo_out(r).start()
+        return carry
 
     def backward(r):
         xhat, scale = normalize(inp_s[r].astype(F32))
         dx = (dn_s[r] + back_s[r].astype(F32)) * gain_ref[...]
-        ig_s[r] = g_s[r].astype(F32) + (dx - jnp.mean(dx, -1, keepdims=True) - xhat * jnp.mean(dx * xhat, -1, keepdims=True)) * scale
+        ig_s[r] = g_s[lax.rem(part_ref[r], 4)].astype(F32) + (dx - jnp.mean(dx, -1, keepdims=True) - xhat * jnp.mean(dx * xhat, -1, keepdims=True)) * scale
         ig_out(r).start()
 
     made[0].tick(1)
     small.tick(1)
     for copy in list(blocks.values()) + loads[:3]:
         copy.wait()
-    forward(0)
-    forward(1)
+    lax.fori_loop(0, 2, forward, 0)
     made[1].tick(1)
-    forward(2)
-    forward(3)
+    lax.fori_loop(2, 4, forward, 0)
     made[0].tick(2)
     made[2].tick(1)
     small.tick(2)
@@ -870,7 +877,7 @@
         ig_out(r).wait()
 
 
-def finish(dat, heads, gq, go, inp, g, y, dn, wo, gain, dbias, sums_ff, sums_at, ub, early):
+def finish(dat, heads, gq, go, inp, cot, y, dn, wo, partners, gain, dbias, sums_ff, sums_at, ub, early):
     sd, vm = jax.ShapeDtypeStruct, pltpu.VMEM
     shape, d = inp.shape, inp.shape[2]
     vmem = pl.BlockSpec(memory_space=pltpu.VMEM)
@@ -878,36 +885,64 @@
         tail_kernel,
         out_shape=[sd(shape, BF16), sd(shape, F32), sd((128, 768), F32), sd((128, 256), F32), sd((1, d), F32), sd((1, d), F32), sd((1, 4 * d), F32),
                    sd((1, d), F32)],
-        in_specs=[ANYWHERE] * 9 + [vmem] * 6, out_specs=[ANYWHERE] * 2 + [vmem] * 6,
+        in_specs=[ANYWHERE] * 9 + [pl.BlockSpec(memory_space=pltpu.SMEM)] + [vmem] * 6, out_specs=[ANYWHERE] * 2 + [vmem] * 6,
         scratch_shapes=[vm(shape, BF16)] * 4 + [vm(shape, F32)] * 2 + [vm((d, d), BF16), vm(shape, BF16), vm(shape, F32),
                         vm((8, d), F32), vm((3, 8, d), F32), vm((4, 8, d), F32),
                         DMA((5,)), DMA((8,)), DMA((3,)), DMA((3,)), DMA((1,)), DMA((6,)), DMA((6,)), DMA((4,)), DMA((4,))]
         + piece_scratch(256, TAIL_SPLITS[0]) + piece_scratch(384, TAIL_SPLITS[1]) + piece_scratch(384, TAIL_SPLITS[2]),
         compiler_params=pltpu.CompilerParams(collective_id=2, has_side_effects=True, vmem_limit_bytes=56 * 2**20),
-    )(dat.reshape(shape), heads, gq, go, inp, g, y.reshape(shape), dn.reshape(shape), wo, gain.reshape(1, d), dbias.reshape(1, d), sums_ff, sums_at,
+    )(dat.reshape(shape), heads, gq, go, inp, cot, y.reshape(shape), dn.reshape(shape), wo, partners, gain.reshape(1, d), dbias.reshape(1, d), sums_ff, sums_at,
       ub, early)
+
+
+def copy_kernel(*refs, moves):
+    count = len(refs) - 1
+    refs, sem = refs[:count], refs[count]
+    copies = [local_copy(refs[a].at[at], refs[b].at[to], sem.at[k]) for k, (a, at, b, to) in enumerate(moves)]
+    for copy in copies:
+        copy.start()
+    for copy in copies:
+        copy.wait()
+
+
+def gather_up(layer_out, input_grad, qkv_sum, out_sum, small, ups, downs):
+    sd, everything = jax.ShapeDtypeStruct, slice(None)
+    ins = [layer_out, input_grad, qkv_sum, out_sum, *small, *ups, *downs]
+    shapes = [sd(layer_out.shape, BF16), sd(input_grad.shape, F32), sd(qkv_sum.shape, F32), sd(out_sum.shape, F32), *[sd(v.shape, F32) for v in small],
+              sd((128, 1024), F32), sd((512, 256), F32)]
+    first = len(ins)
+    moves = [(a, r, first + a, r) for a in (1, 0) for r in range(4)]
+    moves += [(a, (everything, everything), first + a, (everything, everything)) for a in range(2, 8)]
+    for k in range(4):
+        for half in range(2):
+            moves.append((8 + k, (everything, slice(half * 128, half * 128 + 128)), first + 8,
+                          (everything, slice(half * 512 + k * 128, half * 512 + k * 128 + 128))))
+        moves.append((12 + k, (everything, everything), first + 9, (slice(k * 128, k * 128 + 128), everything)))
+    return pl.pallas_call(functools.partial(copy_kernel, moves=moves), out_shape=shapes, in_specs=[ANYWHERE] * first, out_specs=[ANYWHERE] * len(shapes),
+                          scratch_shapes=[DMA((len(moves),))])(*ins)
 
 
 def on_device(inputs, norm_gain, norm_shift, qkv_weight, out_weight, up_weight, up_bias, down_weight, down_bias, partners, families, cotangent, linked):
     row_count, place_count, width = inputs.shape
     tokens = row_count * place_count
-    local_rows = partners - lax.axis_index("dp") * row_count
-    grad = jnp.take(cotangent, local_rows, axis=0, mode="clip")
     branch_args = norm_gain, norm_shift, qkv_weight, out_weight, families, linked
     if linked:
-        y, dn, sums_ff, ub, grads, row_inputs, row_grad, up0, down0, up1, down1 = feed_forward(inputs, grad, norm_gain, norm_shift, up_bias, up_weight, down_weight, True)
+        y, dn, sums_ff, ub, grads, row_inputs, row_grad, up0, down0, up1, down1 = feed_forward(
+            inputs, cotangent, partners, norm_gain, norm_shift, up_bias, up_weight, down_weight, True)
         dat, sums_at, gq, go, heads, up2, down2, up3, down3, early = attend(
             row_inputs.reshape(tokens, width), row_grad.reshape(tokens, width), *branch_args, grads)
         layer_out, input_grad, qkv_sum, out_sum, gain_sum, shift_sum, ub_sum, db_sum = finish(
-            dat, heads, gq, go, inputs, grad, y, dn, out_weight, norm_gain, down_bias, sums_ff, sums_at, ub, early)
-        ups = (up0, up1, up2, up3)
-        up_sum = jnp.concatenate([u[:, :128] for u in ups] + [u[:, 128:] for u in ups], 1)
-        down_sum = jnp.concatenate([down0, down1, down2, down3], 0)
+            dat, heads, gq, go, inputs, cotangent, y, dn, out_weight, partners, norm_gain, down_bias, sums_ff, sums_at, ub, early)
+        layer_out, input_grad, qkv_sum, out_sum, gain_sum, shift_sum, ub_sum, db_sum, up_sum, down_sum = gather_up(
+            layer_out, input_grad, qkv_sum, out_sum, (gain_sum, shift_sum, ub_sum, db_sum), (up0, up1, up2, up3), (down0, down1, down2, down3))
         return (layer_out, input_grad, gain_sum.reshape(width), shift_sum.reshape(width), qkv_sum, out_sum, up_sum, ub_sum.reshape(-1), down_sum,
                 db_sum.reshape(width))
+    local_rows = partners - lax.axis_index("dp") * row_count
+    grad = jnp.take(cotangent, local_rows, axis=0, mode="clip")
     swap = functools.partial(lax.all_to_all, axis_name="seq", split_axis=0, concat_axis=0, tiled=True)
     row_inputs, row_grad = swap(inputs).reshape(tokens, width), swap(grad).reshape(tokens, width)
-    y, dn, sums_ff, ub, up_grad, down_grad = feed_forward(inputs, grad, norm_gain, norm_shift, up_bias, up_weight, down_weight, False)
+    y, dn, sums_ff, ub, up_grad, down_grad = feed_forward(
+        inputs, cotangent, partners, norm_gain, norm_shift, up_bias, up_weight, down_weight, False)
     dat, sums_at, qkv_grad, out_grad, heads = attend(row_inputs, row_grad, *branch_args)
 
     def scatter(parts, columns):

time: 251 us -> 476 us (1.90)
  Pallas kernels: 236 us -> 475 us
  local copies, waits for them, and re-layouts: 12.7 us -> 0 us
    pallas_call x0 -> x1, Pallas kernels: none -> 240 us  [gather_up(): pl.pallas_call(functools.partial(copy_kernel, moves=moves), out_shape=sha...]
    unnamed x53 -> x0, local copies, waits for them, and re-layouts: 10.7 us -> none
where the time goes in v1:
time: 476 us
  Pallas kernels  475 us (100%)
    pallas_call x1, Pallas kernels, gather_up(): pl.pallas_call(functools.partial(copy_kernel, moves=moves), out_shape=sha...  240 us
    pallas_call x1, Pallas kernels, feed_forward(): pl.pallas_call(functools.partial(ff_kernel, linked=linked), out_shape=out...  93.8 us
    pallas_call x1, Pallas kernels, attend(): pl.pallas_call(functools.partial(attn_kernel, linked=linked), out_shape=o...  93.7 us
    pallas_call x1, Pallas kernels, finish(): pl.pallas_call(tail_kernel, out_shape=[sd(shape, BF16), sd(shape, F32), s...  46.8 us

profile of v1, /device:TPU:0, one launch (start us, length us, event | category | flops | bytes accessed | tf_op | source)
XLA Modules:
  0.0 475.5 jit_solution(5588841888607918645)
XLA Ops:
  0.6 93.8 %shard_map.204 = (f32[1024,1024]{1,0:T(8,128)}, f32[1024,1024]{1,0:T(8,128)}, f32[8,1024]{1,0:T(8,128)}, f32[1,4096]{1,0:T(1,128)}, bf16[4,4,2,256,1024]{4,3,2,1...) custom-call(s32[4]{0:T(128)} %part_ref.3, ...), custom_call_target="tpu_custom_call" | custom-call | flops 51999997952 | bytes 50000000 | tf_op jit(solution)/shard_map/pallas_call | solution.py:409
  94.4 93.7 %shard_map.205 = (bf16[1024,1024]{1,0:T(8,128)(2,1)}, f32[8,1024]{1,0:T(8,128)}, bf16[2,4,2,128,1536]{4,3,2,1,0:T(8,128)(2,1)}, bf16[4,2,128,1024]{3,2,1,0:T(8,1...) custom-call(bf16[1024,1024]{1,0:T(8,128)(2,1)} %bitcast.29, ...), custom_call_target="tpu_custom_call" | custom-call | flops 70000001024 | bytes 30000000 | tf_op jit(solution)/shard_map/pallas_call | solution.py:727
  188.1 46.8 %shard_map.206 = (bf16[4,256,1024]{2,1,0:T(8,128)(2,1)}, f32[4,256,1024]{2,1,0:T(8,128)}, f32[128,768]{1,0:T(8,128)}, f32[128,256]{1,0:T(8,128)}, f32[1,1024]{1,...) custom-call(bf16[4,256,1024]{2,1,0:T(8,128)(2,1)} %bitcast.17, ...), custom_call_target="tpu_custom_call" | custom-call | tf_op jit(solution)/shard_map/pallas_call | solution.py:884
  234.9 240.5 %shard_map.207 = (bf16[4,256,1024]{2,1,0:T(8,128)(2,1)}, f32[4,256,1024]{2,1,0:T(8,128)}, f32[128,768]{1,0:T(8,128)}, f32[128,256]{1,0:T(8,128)}, f32[1,1024]{1,...) custom-call(bf16[4,256,1024]{2,1,0:T(8,128)(2,1)} %get-tuple-element, ...), custom_call_target="tpu_custom_call" | custom-call | tf_op jit(solution)/shard_map/pallas_call | solution.py:921

commit v2 on v1

--- a/solution.py
+++ b/solution.py
@@ -895,31 +895,32 @@
       ub, early)
 
 
-def copy_kernel(*refs, moves):
-    count = len(refs) - 1
-    refs, sem = refs[:count], refs[count]
-    copies = [local_copy(refs[a].at[at], refs[b].at[to], sem.at[k]) for k, (a, at, b, to) in enumerate(moves)]
-    for copy in copies:
-        copy.start()
-    for copy in copies:
-        copy.wait()
-
-
-def gather_up(layer_out, input_grad, qkv_sum, out_sum, small, ups, downs):
-    sd, everything = jax.ShapeDtypeStruct, slice(None)
-    ins = [layer_out, input_grad, qkv_sum, out_sum, *small, *ups, *downs]
-    shapes = [sd(layer_out.shape, BF16), sd(input_grad.shape, F32), sd(qkv_sum.shape, F32), sd(out_sum.shape, F32), *[sd(v.shape, F32) for v in small],
-              sd((128, 1024), F32), sd((512, 256), F32)]
-    first = len(ins)
-    moves = [(a, r, first + a, r) for a in (1, 0) for r in range(4)]
-    moves += [(a, (everything, everything), first + a, (everything, everything)) for a in range(2, 8)]
-    for k in range(4):
-        for half in range(2):
-            moves.append((8 + k, (everything, slice(half * 128, half * 128 + 128)), first + 8,
-                          (everything, slice(half * 512 + k * 128, half * 512 + k * 128 + 128))))
-        moves.append((12 + k, (everything, everything), first + 9, (slice(k * 128, k * 128 + 128), everything)))
-    return pl.pallas_call(functools.partial(copy_kernel, moves=moves), out_shape=shapes, in_specs=[ANYWHERE] * first, out_specs=[ANYWHERE] * len(shapes),
-                          scratch_shapes=[DMA((len(moves),))])(*ins)
+def copy_kernel(*refs):
+    (lo, ig, qkv, out, gain, shift, ub, db), ups, downs = refs[:8], refs[8:12], refs[12:16]
+    lo_o, ig_o, qkv_o, out_o, gain_o, shift_o, ub_o, db_o, up_o, down_o = refs[16:]
+    lo_o[...] = lo[...]
+    ig_o[...] = ig[...]
+
+    @pl.when(pl.program_id(0) == 0)
+    def _():
+        for to, source in ((qkv_o, qkv), (out_o, out), (gain_o, gain), (shift_o, shift), (ub_o, ub), (db_o, db)):
+            to[...] = source[...]
+        for k in range(4):
+            up_o[:, k * 128:(k + 1) * 128] = ups[k][:, 0:128]
+            up_o[:, 512 + k * 128:512 + (k + 1) * 128] = ups[k][:, 128:256]
+            down_o[k * 128:(k + 1) * 128, :] = downs[k][...]
+
+
+def gather_up(*parts):
+    sd, shape = jax.ShapeDtypeStruct, parts[0].shape
+    flat = [(shape[0] * shape[1], shape[2])] * 2 + [p.shape for p in parts[2:]]
+    band = pl.BlockSpec((128, shape[2]), lambda p: (p, 0))
+    outs = flat[:8] + [(128, 1024), (512, 256)]
+    return pl.pallas_call(
+        copy_kernel, out_shape=[sd(s, BF16 if k == 0 else F32) for k, s in enumerate(outs)], grid=(flat[0][0] // 128,),
+        in_specs=[band, band] + [whole(s) for s in flat[2:]], out_specs=[band, band] + [whole(s) for s in outs[2:]],
+        compiler_params=pltpu.CompilerParams(vmem_limit_bytes=32 * 2**20),
+    )(*[p.reshape(s) for p, s in zip(parts, flat)])
 
 
 def on_device(inputs, norm_gain, norm_shift, qkv_weight, out_weight, up_weight, up_bias, down_weight, down_bias, partners, families, cotangent, linked):
@@ -934,9 +935,9 @@
         layer_out, input_grad, qkv_sum, out_sum, gain_sum, shift_sum, ub_sum, db_sum = finish(
             dat, heads, gq, go, inputs, cotangent, y, dn, out_weight, partners, norm_gain, down_bias, sums_ff, sums_at, ub, early)
         layer_out, input_grad, qkv_sum, out_sum, gain_sum, shift_sum, ub_sum, db_sum, up_sum, down_sum = gather_up(
-            layer_out, input_grad, qkv_sum, out_sum, (gain_sum, shift_sum, ub_sum, db_sum), (up0, up1, up2, up3), (down0, down1, down2, down3))
-        return (layer_out, input_grad, gain_sum.reshape(width), shift_sum.reshape(width), qkv_sum, out_sum, up_sum, ub_sum.reshape(-1), down_sum,
-                db_sum.reshape(width))
+            layer_out, input_grad, qkv_sum, out_sum, gain_sum, shift_sum, ub_sum, db_sum, up0, up1, up2, up3, down0, down1, down2, down3)
+        return (layer_out.reshape(inputs.shape), input_grad.reshape(inputs.shape), gain_sum.reshape(width), shift_sum.reshape(width), qkv_sum, out_sum,
+                up_sum, ub_sum.reshape(-1), down_sum, db_sum.reshape(width))
     local_rows = partners - lax.axis_index("dp") * row_count
     grad = jnp.take(cotangent, local_rows, axis=0, mode="clip")
     swap = functools.partial(lax.all_to_all, axis_name="seq", split_axis=0, concat_axis=0, tiled=True)

time: 476 us -> 249 us (0.52)
  Pallas kernels: 475 us -> 239 us
  local copies, waits for them, and re-layouts: 0 us -> 8.45 us
    pallas_call x1, Pallas kernels: 240 us -> 4.6 us  [gather_up(): pl.pallas_call(copy_kernel, out_shape=[sd(s, BF16 if k == 0 else F32) for...]
    unnamed x0 -> x32, local copies, waits for them, and re-layouts: none -> 8.45 us
where the time goes in v2:
time: 249 us; the launch traced here: 248 us
  Pallas kernels  239 us (96%)
  local copies, waits for them, and re-layouts  8.45 us (3%)
    pallas_call x1, Pallas kernels, feed_forward(): pl.pallas_call(functools.partial(ff_kernel, linked=linked), out_shape=out...  93.8 us
    pallas_call x1, Pallas kernels, attend(): pl.pallas_call(functools.partial(attn_kernel, linked=linked), out_shape=o...  93.6 us
    pallas_call x1, Pallas kernels, finish(): pl.pallas_call(tail_kernel, out_shape=[sd(shape, BF16), sd(shape, F32), s...  46.9 us
    unnamed x32, local copies, waits for them, and re-layouts  8.45 us

profile of v2, /device:TPU:0, one launch (start us, length us, event | category | flops | bytes accessed | tf_op | source)
XLA Modules:
  0.0 248.4 jit_solution(17975733934610170361)
XLA Ops:
  0.6 93.8 %shard_map.204 = (f32[1024,1024]{1,0:T(8,128)}, f32[1024,1024]{1,0:T(8,128)}, f32[8,1024]{1,0:T(8,128)}, f32[1,4096]{1,0:T(1,128)}, bf16[4,4,2,256,1024]{4,3,2,1...) custom-call(s32[4]{0:T(128)} %part_ref.3, ...), custom_call_target="tpu_custom_call" | custom-call | flops 51999997952 | bytes 50000000 | tf_op jit(solution)/shard_map/pallas_call | solution.py:409
  94.4 93.6 %shard_map.205 = (bf16[1024,1024]{1,0:T(8,128)(2,1)}, f32[8,1024]{1,0:T(8,128)}, bf16[2,4,2,128,1536]{4,3,2,1,0:T(8,128)(2,1)}, bf16[4,2,128,1024]{3,2,1,0:T(8,1...) custom-call(bf16[1024,1024]{1,0:T(8,128)(2,1)} %bitcast.37, ...), custom_call_target="tpu_custom_call" | custom-call | flops 70000001024 | bytes 30000000 | tf_op jit(solution)/shard_map/pallas_call | solution.py:727
  188.1 0.0 copy-start.3
  188.1 0.0 copy-start.4
  188.1 0.0 copy-start.5
  188.1 0.0 copy-start.6
  188.1 0.0 copy-start.7
  188.1 0.0 copy-start.8
  188.1 0.0 copy-start.9
  188.1 0.0 copy-start.10
  188.1 46.9 %shard_map.206 = (bf16[4,256,1024]{2,1,0:T(8,128)(2,1)}, f32[4,256,1024]{2,1,0:T(8,128)}, f32[128,768]{1,0:T(8,128)}, f32[128,256]{1,0:T(8,128)}, f32[1,1024]{1,...) custom-call(bf16[4,256,1024]{2,1,0:T(8,128)(2,1)} %bitcast.23, ...), custom_call_target="tpu_custom_call" | custom-call | tf_op jit(solution)/shard_map/pallas_call | solution.py:884
  235.1 0.0 copy-done.3
  235.1 0.0 copy-done.4
  235.1 0.0 copy-done.5
  235.1 0.0 copy-done.6
  235.1 0.0 copy-done.7
  235.1 0.0 copy-done.8
  235.1 0.0 copy-done.9
  235.1 0.0 copy-done.10
  235.2 0.0 copy-start
  235.2 2.2 copy-done
  237.3 0.0 copy-start.1
  237.3 1.6 copy-done.1
  238.9 0.0 copy-start.2
  238.9 1.0 copy-done.2
  239.9 0.0 copy-start.11
  239.9 0.9 copy-done.11
  240.8 0.0 copy-start.12
  240.8 0.7 copy-done.12
  241.6 0.0 copy-start.13
  241.6 0.7 copy-done.13
  242.2 0.0 copy-start.14
  242.2 0.7 copy-done.14
  242.9 0.0 copy-start.15
  242.9 0.7 copy-done.15
  243.6 4.6 %shard_map.207 = (bf16[1024,1024]{1,0:T(8,128)(2,1)}, f32[1024,1024]{1,0:T(8,128)}, f32[128,768]{1,0:T(8,128)}, f32[128,256]{1,0:T(8,128)}, f32[1,1024]{1,0:T(1,...) custom-call(bf16[1024,1024]{1,0:T(8,128)(2,1)S(1)} %bitcast.19, ...), custom_call_target="tpu_custom_call" | custom-call | tf_op jit(solution)/shard_map/pallas_call | solution.py:919
Async XLA Ops:
  188.1 47.0 %copy-start.3 = (f32[128,256]{1,0:T(8,128)S(1)}, f32[128,256]{1,0:T(8,128)}, u32[]{:S(2)}) copy-start(f32[128,256]{1,0:T(8,128)} %get-tuple-element.70.refs_8_) | copy-start | bytes 393220
  188.1 47.0 %copy-start.4 = (f32[128,256]{1,0:T(8,128)S(1)}, f32[128,256]{1,0:T(8,128)}, u32[]{:S(2)}) copy-start(f32[128,256]{1,0:T(8,128)} %get-tuple-element.74.refs_12_) | copy-start | bytes 393220
  188.1 47.0 %copy-start.5 = (f32[128,256]{1,0:T(8,128)S(1)}, f32[128,256]{1,0:T(8,128)}, u32[]{:S(2)}) copy-start(f32[128,256]{1,0:T(8,128)} %get-tuple-element.71.refs_9_) | copy-start | bytes 393220
  188.1 47.0 %copy-start.6 = (f32[128,256]{1,0:T(8,128)S(1)}, f32[128,256]{1,0:T(8,128)}, u32[]{:S(2)}) copy-start(f32[128,256]{1,0:T(8,128)} %get-tuple-element.75.refs_13_) | copy-start | bytes 393220
  188.1 47.0 %copy-start.7 = (f32[128,256]{1,0:T(8,128)S(1)}, f32[128,256]{1,0:T(8,128)}, u32[]{:S(2)}) copy-start(f32[128,256]{1,0:T(8,128)} %get-tuple-element.72.refs_10_) | copy-start | bytes 393220
  188.1 47.0 %copy-start.8 = (f32[128,256]{1,0:T(8,128)S(1)}, f32[128,256]{1,0:T(8,128)}, u32[]{:S(2)}) copy-start(f32[128,256]{1,0:T(8,128)} %get-tuple-element.76.refs_14_) | copy-start | bytes 393220
  188.1 47.0 %copy-start.9 = (f32[128,256]{1,0:T(8,128)S(1)}, f32[128,256]{1,0:T(8,128)}, u32[]{:S(2)}) copy-start(f32[128,256]{1,0:T(8,128)} %get-tuple-element.73.refs_11_) | copy-start | bytes 393220
  188.1 47.0 %copy-start.10 = (f32[128,256]{1,0:T(8,128)S(1)}, f32[128,256]{1,0:T(8,128)}, u32[]{:S(2)}) copy-start(f32[128,256]{1,0:T(8,128)} %get-tuple-element.77.refs_15_) | copy-start | bytes 393220
  235.2 2.2 copy-start
  237.3 1.6 copy-start.1
  238.9 1.0 copy-start.2
  239.9 0.9 copy-start.11
  240.8 0.7 copy-start.12
  241.6 0.7 copy-start.13
  242.2 0.7 copy-start.14
  242.9 0.7 copy-start.15

commit v3 on v2

--- a/solution.py
+++ b/solution.py
@@ -919,7 +919,7 @@
     return pl.pallas_call(
         copy_kernel, out_shape=[sd(s, BF16 if k == 0 else F32) for k, s in enumerate(outs)], grid=(flat[0][0] // 128,),
         in_specs=[band, band] + [whole(s) for s in flat[2:]], out_specs=[band, band] + [whole(s) for s in outs[2:]],
-        compiler_params=pltpu.CompilerParams(vmem_limit_bytes=32 * 2**20),
+        compiler_params=pltpu.CompilerParams(vmem_limit_bytes=60 * 2**20),
     )(*[p.reshape(s) for p, s in zip(parts, flat)])
 
 

time: 249 us -> 244 us (0.980)
  local copies, waits for them, and re-layouts: 8.45 us -> 0 us
  Pallas kernels: 239 us -> 243 us
    unnamed x32 -> x0, local copies, waits for them, and re-layouts: 8.45 us -> none
    pallas_call x1, Pallas kernels: 4.6 us -> 8.95 us  [gather_up(): pl.pallas_call(copy_kernel, out_shape=[sd(s, BF16 if k == 0 else F32) for...]
where the time goes in v3:
time: 244 us
  Pallas kernels  243 us (100%)
    pallas_call x1, Pallas kernels, feed_forward(): pl.pallas_call(functools.partial(ff_kernel, linked=linked), out_shape=out...  93.8 us
    pallas_call x1, Pallas kernels, attend(): pl.pallas_call(functools.partial(attn_kernel, linked=linked), out_shape=o...  93.7 us
    pallas_call x1, Pallas kernels, finish(): pl.pallas_call(tail_kernel, out_shape=[sd(shape, BF16), sd(shape, F32), s...  46.8 us
    pallas_call x1, Pallas kernels, gather_up(): pl.pallas_call(copy_kernel, out_shape=[sd(s, BF16 if k == 0 else F32) for...  8.95 us

profile of v3, /device:TPU:0, one launch (start us, length us, event | category | flops | bytes accessed | tf_op | source)
XLA Modules:
  0.0 244.0 jit_solution(7618795729559533403)
XLA Ops:
  0.6 93.8 %shard_map.204 = (f32[1024,1024]{1,0:T(8,128)}, f32[1024,1024]{1,0:T(8,128)}, f32[8,1024]{1,0:T(8,128)}, f32[1,4096]{1,0:T(1,128)}, bf16[4,4,2,256,1024]{4,3,2,1...) custom-call(s32[4]{0:T(128)} %part_ref.3, ...), custom_call_target="tpu_custom_call" | custom-call | flops 51999997952 | bytes 50000000 | tf_op jit(solution)/shard_map/pallas_call | solution.py:409
  94.4 93.7 %shard_map.205 = (bf16[1024,1024]{1,0:T(8,128)(2,1)}, f32[8,1024]{1,0:T(8,128)}, bf16[2,4,2,128,1536]{4,3,2,1,0:T(8,128)(2,1)}, bf16[4,2,128,1024]{3,2,1,0:T(8,1...) custom-call(bf16[1024,1024]{1,0:T(8,128)(2,1)} %bitcast.37, ...), custom_call_target="tpu_custom_call" | custom-call | flops 70000001024 | bytes 30000000 | tf_op jit(solution)/shard_map/pallas_call | solution.py:727
  188.1 46.8 %shard_map.206 = (bf16[4,256,1024]{2,1,0:T(8,128)(2,1)}, f32[4,256,1024]{2,1,0:T(8,128)}, f32[128,768]{1,0:T(8,128)}, f32[128,256]{1,0:T(8,128)}, f32[1,1024]{1,...) custom-call(bf16[4,256,1024]{2,1,0:T(8,128)(2,1)} %bitcast.22, ...), custom_call_target="tpu_custom_call" | custom-call | tf_op jit(solution)/shard_map/pallas_call | solution.py:884
  234.9 9.0 %shard_map.207 = (bf16[1024,1024]{1,0:T(8,128)(2,1)}, f32[1024,1024]{1,0:T(8,128)}, f32[128,768]{1,0:T(8,128)}, f32[128,256]{1,0:T(8,128)}, f32[1,1024]{1,0:T(1,...) custom-call(bf16[1024,1024]{1,0:T(8,128)(2,1)} %bitcast.23, ...), custom_call_target="tpu_custom_call" | custom-call | tf_op jit(solution)/shard_map/pallas_call | solution.py:919

commit v4 on v3

--- a/solution.py
+++ b/solution.py
@@ -16,12 +16,13 @@
 C0 = 0.7978845608028654
 C1 = C0 * 0.044715
 TILE = 256
-FF_SPLITS = (0, 176, 80), (96, 112, 48)
-AT_SPLIT = 96, 112, 48
+FF_SPLIT = 0, 176, 80
+AT_SPLIT = 64, 128, 64
 EARLY_SPLIT = 48, 64, 16
+TAIL_FIRST = 2
 TAIL_SPLITS = (0, 80, 48), (0, 48, 16), (0, 32, 32)
-FF_TICKS = (6, 9, 15, 18, 22), (12, 15, 20, 22, 24)
-AT_TICKS = (0, 2, 7, 10, 14), (4, 7, 12, 15, 19), (13, 15, 19, 21, 24)
+FF_TICKS = 6, 10, 18, 21, 24
+AT_TICKS = (0, 2, 7, 10, 14), (4, 7, 12, 15, 19), (8, 12, 17, 20, 23), (13, 17, 21, 23, 24)
 ORDER = ((0, 3), (4, 7), (1, 2), (5, 6))
 MESH_ID = pl.DeviceIdType.MESH
 ANYWHERE = pl.BlockSpec(memory_space=pl.ANY)
@@ -217,23 +218,25 @@
             self.done(jnp.concatenate(parts, 0) if len(parts) > 1 else parts[0])
 
 
+def hidden_runs(at, hidden):
+    return [(s, (2 * s + at % 2) * (hidden // 8) + at // 2 * 128) for s in range(4)]
+
+
 def ff_kernel(part_ref, inp_ref, cot_ref, gain_ref, shift_ref, bias_ref, wu_ref, wd_ref, *rest, linked):
     hand, rest = (rest[:1], rest[1:]) if linked else ((), rest)
     y_ref, dn_ref, sums_ref, ub_ref = rest[:4]
-    outs, rest = (rest[4:11], rest[11:]) if linked else (rest[4:6], rest[6:])
-    x_s, xt_s, act_s, dh_s, wu_s, wd_s, gu_s, gd_s, g_ref, wu_sem, wd_sem, gu_sem, gd_sem = rest[:13]
-    rest = rest[13:]
+    outs, rest = (rest[4:9], rest[9:]) if linked else (rest[4:6], rest[6:])
+    x_s, xt_s, act_s, dh_s, wu_s, wd_s, gu_s, gd_s, g_ref, wu_sem, wd_sem, gu_sem, gd_sem, act_sem = rest[:14]
+    rest = rest[14:]
     step = pl.program_id(0)
     last = pl.num_programs(0) - 1
     n, d = x_s.shape
     hidden = bias_ref.shape[1]
-    group = hidden // 8
     tile = 512
     slot = step % 2
 
     def places(at):
-        k, j = at // 2, at % 2
-        return [(s, (2 * s + j) * group + k * 128) for s in range(4)]
+        return hidden_runs(at, hidden)
 
     def weights(at, slot):
         out = []
@@ -258,6 +261,9 @@
             out.append(local_copy(down, to[1], gd_sem.at[s]))
         return out
 
+    def keep(at):
+        return [local_copy(act_s, y_ref.at[at], act_sem.at[0])] if linked else []
+
     if linked:
         place = Place()
         row_send, row_recv, own_sem = rest[:3]
@@ -282,11 +288,10 @@
                 outs[4 + 2 * k][...] = total[128:256]
             return done
 
-        cut = piece_count(FF_SPLITS[0])
-        made = [Piece(place, part_of(k), done_at(k), FF_SPLITS[k], (rest[:cut], rest[cut:])[k]) for k in range(2)]
+        made = [Piece(place, part_of(0), done_at(0), FF_SPLIT, rest)]
 
     def tick(position):
-        for which, times in enumerate(FF_TICKS if linked else ()):
+        for which, times in enumerate((FF_TICKS,) if linked else ()):
             for t, at in enumerate(times):
                 if min(at // 3, 7) * 3 + position == at:
                     pl.when(step == min(at // 3, 7))(functools.partial(made[which].tick, t))
@@ -317,7 +322,7 @@
 
     @pl.when(step > 0)
     def _():
-        for copy in results(step - 1):
+        for copy in results(step - 1) + keep(step - 1):
             copy.wait()
 
     tick(0)
@@ -343,6 +348,8 @@
         dh_s[here, :] = dh
         total = jnp.sum(dh.astype(F32), 0, keepdims=True)
         unit_sums = total if unit_sums is None else unit_sums + total
+    for copy in keep(step):
+        copy.start()
     for s, f in places(step):
         ub_ref[:, pl.ds(pl.multiple_of(f, 128), 128)] = unit_sums[:, s * 128:(s + 1) * 128]
 
@@ -357,17 +364,19 @@
     tick(2)
     for m in range(n // tile):
         here = slice(m * tile, (m + 1) * tile)
-        y = dot(act_s[here, :], w_down[...])
+        y = None if linked else dot(act_s[here, :], w_down[...])
         dn = dot_nt(dh_s[here, :], w_up[...])
 
         @pl.when(step == 0)
         def _():
-            y_ref[here, :] = y
+            if not linked:
+                y_ref[here, :] = y
             dn_ref[here, :] = dn
 
         @pl.when(step > 0)
         def _():
-            y_ref[here, :] += y
+            if not linked:
+                y_ref[here, :] += y
             dn_ref[here, :] += dn
 
     tick(3)
@@ -381,7 +390,7 @@
             sums_ref[0:1, :] += jnp.sum(total * xhat, 0, keepdims=True)
             sums_ref[1:2, :] += jnp.sum(total, 0, keepdims=True)
 
-        for copy in results(step):
+        for copy in results(step) + keep(step):
             copy.wait()
         if linked:
             for copy in swaps(0) + swaps(1):
@@ -392,16 +401,16 @@
     rows, span, d = inp.shape
     n, hidden = rows * span, bias.shape[0]
     sd, vm = jax.ShapeDtypeStruct, pltpu.VMEM
-    out_shape = [sd((n, d), F32), sd((n, d), F32), sd((8, d), F32), sd((1, hidden), F32)]
-    out_specs = [whole((n, d)), whole((n, d)), whole((8, d)), whole((1, hidden))]
+    out_shape = [sd((hidden // 512, n, 512), BF16) if linked else sd((n, d), F32), sd((n, d), F32), sd((8, d), F32), sd((1, hidden), F32)]
+    out_specs = [ANYWHERE if linked else whole((n, d)), whole((n, d)), whole((8, d)), whole((1, hidden))]
     scratch = [vm((n, d), BF16), vm((d, n), BF16), vm((n, 512), BF16), vm((n, 512), BF16), vm((2, d, 512), BF16), vm((2, 512, d), BF16),
-               vm((4, 2, 128, 512), BF16), vm((512, d), BF16), vm((n, d), BF16), DMA((2, 4)), DMA((2, 4)), DMA((4,)), DMA((4,))]
+               vm((4, 2, 128, 512), BF16), vm((512, d), BF16), vm((n, d), BF16), DMA((2, 4)), DMA((2, 4)), DMA((4,)), DMA((4,)), DMA((1,))]
     more, params = [], {}
     if linked:
         more = [inp]
-        out_shape += [sd((4, 4, 2, 256, d), BF16), sd(inp.shape, BF16), sd(inp.shape, BF16), *[sd((128, 256), F32)] * 4]
-        out_specs += [ANYWHERE] * 3 + [whole((128, 256))] * 4
-        scratch += [DMA((2, 3)), DMA((2, 3)), DMA((2,))] + piece_scratch(256, FF_SPLITS[0]) + piece_scratch(256, FF_SPLITS[1])
+        out_shape += [sd((4, 4, 2, 256, d), BF16), sd(inp.shape, BF16), sd(inp.shape, BF16), *[sd((128, 256), F32)] * 2]
+        out_specs += [ANYWHERE] * 3 + [whole((128, 256))] * 2
+        scratch += [DMA((2, 3)), DMA((2, 3)), DMA((2,))] + piece_scratch(256, FF_SPLIT)
         params = dict(collective_id=0, has_side_effects=True)
     else:
         out_shape += [sd((4, 2, 128, hidden), BF16), sd((hidden, d), BF16)]
@@ -432,7 +441,7 @@
 def attn_kernel(raw_ref, g_ref, gain_ref, shift_ref, fam_ref, tab_ref, wqkv_ref, wo_ref, *rest, linked):
     hand, rest = (rest[:1], rest[1:]) if linked else ((), rest)
     dn_ref, sums_ref, gqkv_ref, go_ref, heads_ref = rest[:5]
-    outs, rest = (rest[5:10], rest[10:]) if linked else ((), rest[5:])
+    outs, rest = (rest[5:12], rest[12:]) if linked else ((), rest[5:])
     (x_s, xt_s, c_s, s_s, w_s, wo_s, q_s, k_s, v_s, do_s, kt_s, vt_s, ht_s, dqt_s, dk_s, dv_s, draw_s, dn_s, gq_s, go_s, heads_s,
      famr_s, famc_s, w_sem, wo_sem, gq_sem, go_sem, h_sem) = rest[:28]
     rest = rest[28:]
@@ -491,17 +500,16 @@
 
         def done_at(k):
             def done(total):
-                if k == 2:
-                    outs[4][...] = total
+                if k == 3:
+                    outs[6][...] = total
                 else:
                     outs[2 * k][...] = total[0:128]
                     outs[2 * k + 1][...] = total[128:256]
             return done
 
         cut = piece_count(AT_SPLIT)
-        made = [Piece(place, part_of(hand[0], 2, 256), done_at(0), AT_SPLIT, rest[:cut]),
-                Piece(place, part_of(hand[0], 3, 256), done_at(1), AT_SPLIT, rest[cut:2 * cut]),
-                Piece(place, part_of(gqkv_ref, 0, 384), done_at(2), EARLY_SPLIT, rest[2 * cut:])]
+        made = [Piece(place, part_of(hand[0], 1 + k, 256), done_at(k), AT_SPLIT, rest[k * cut:(k + 1) * cut]) for k in range(3)]
+        made.append(Piece(place, part_of(gqkv_ref, 0, 384), done_at(3), EARLY_SPLIT, rest[3 * cut:]))
         plan = {}
         for which, times in enumerate(AT_TICKS):
             for t, at in enumerate(times):
@@ -719,10 +727,10 @@
     params, more = {}, []
     if linked:
         more = [grads]
-        out_shape += [sd((128, 256), F32)] * 4 + [sd((128, 384), F32)]
-        out_specs += [whole((128, 256))] * 4 + [whole((128, 384))]
+        out_shape += [sd((128, 256), F32)] * 6 + [sd((128, 384), F32)]
+        out_specs += [whole((128, 256))] * 6 + [whole((128, 384))]
         scratch += [DMA((4, 3)), DMA((4, 3))]
-        scratch += piece_scratch(256, AT_SPLIT) * 2 + piece_scratch(384, EARLY_SPLIT)
+        scratch += piece_scratch(256, AT_SPLIT) * 3 + piece_scratch(384, EARLY_SPLIT)
         params = dict(collective_id=1, has_side_effects=True)
     return pl.pallas_call(
         functools.partial(attn_kernel, linked=linked), out_shape=out_shape, grid=(len(ORDER),),
@@ -762,9 +770,9 @@
         return None if t < 4 else self.by_z[0] + self.by_z[1] + self.by_z[2] + self.by_z[3]
 
 
-def tail_kernel(dat_ref, heads_ref, gq_ref, go_ref, inp_ref, cot_ref, y_ref, dn_ref, wo_ref, part_ref, gain_ref, dbias_ref, sums_ff_ref, sums_at_ref,
+def tail_kernel(dat_ref, heads_ref, gq_ref, go_ref, inp_ref, cot_ref, act_ref, wd_ref, dn_ref, wo_ref, part_ref, gain_ref, dbias_ref, sums_ff_ref, sums_at_ref,
                 ub_ref, early_ref, lo_ref, ig_ref, qkv_ref, out_ref, gain_o, shift_o, ub_o, db_o,
-                back_s, inp_s, g_s, heads_s, y_s, dn_s, wo_s, lo_s, ig_s, small_s, heard_s, by_z_s,
+                back_s, inp_s, g_s, heads_s, y_s, dn_s, wo_s, lo_s, ig_s, small_s, heard_s, by_z_s, act_s, wd_s, act_sem, wd_sem,
                 load_sem, wo_sem, back_send, back_recv, own_sem, small_send, small_recv, lo_sem, ig_sem, *pieces):
     place = Place()
     d = wo_s.shape[0]
@@ -811,7 +819,7 @@
         copy.start()
     small.tick(0)
     loads = [local_copy(a, b, load_sem.at[k]) for k, (a, b) in enumerate(
-        ((heads_ref, heads_s), (inp_ref, inp_s), (y_ref, y_s), (cot_ref, g_s), (dn_ref, dn_s)))]
+        ((heads_ref, heads_s), (inp_ref, inp_s), (cot_ref, g_s), (dn_ref, dn_s)))]
     for pair in range(d // 128):
         at = [p for two in ORDER for p in two].index(pair)
         blocks[at] = local_copy(wo_ref.at[pl.ds(pair * 128, 128), :], wo_s.at[pl.ds(at * 128, 128), :], wo_sem.at[at])
@@ -825,7 +833,7 @@
         return local_copy(ig_s.at[r], ig_ref.at[r], ig_sem.at[r])
 
     def forward(r, carry):
-        total = inp_s[r].astype(F32) + dot(heads_s[r], wo_s[...]) + (y_s[r] + dbias_ref[...])
+        total = inp_s[r].astype(F32) + dot(heads_s[r], wo_s[...]) + y_s[r]
         lo_s[r] = total.astype(BF16)
         lo_out(r).start()
         return carry
@@ -836,34 +844,68 @@
         ig_s[r] = g_s[lax.rem(part_ref[r], 4)].astype(F32) + (dx - jnp.mean(dx, -1, keepdims=True) - xhat * jnp.mean(dx * xhat, -1, keepdims=True)) * scale
         ig_out(r).start()
 
-    made[0].tick(1)
-    small.tick(1)
-    for copy in list(blocks.values()) + loads[:3]:
+    hidden = wd_ref.shape[0]
+    chunks = hidden // 512
+
+    def chunk(at, slot):
+        out = [local_copy(act_ref.at[at], act_s.at[slot], act_sem.at[slot])]
+        for k, f in hidden_runs(at, hidden):
+            f = pl.multiple_of(f, 128)
+            out.append(local_copy(wd_ref.at[pl.ds(f, 128), :], wd_s.at[slot, pl.ds(k * 128, 128), :], wd_sem.at[slot, k]))
+        return out
+
+    for copy in chunk(0, 0):
+        copy.start()
+
+    def down(at, carry):
+        slot = at % 2
+
+        @pl.when(at + 1 < chunks)
+        def _():
+            for copy in chunk(at + 1, 1 - slot):
+                copy.start()
+
+        @pl.when(at == TAIL_FIRST)
+        def _():
+            for piece in made:
+                piece.tick(1)
+            small.tick(1)
+
+        @pl.when(at == TAIL_FIRST + 4)
+        def _():
+            small.tick(2)
+
+        for copy in chunk(at, slot):
+            copy.wait()
+        for r in range(4):
+            y_s[r] += dot(act_s[slot, r * 256:(r + 1) * 256, :], wd_s[slot])
+        return carry
+
+    for r in range(4):
+        y_s[r] = jnp.broadcast_to(dbias_ref[...], y_s.shape[1:])
+    lax.fori_loop(0, chunks, down, 0)
+    for copy in list(blocks.values()) + loads[:2]:
         copy.wait()
     lax.fori_loop(0, 2, forward, 0)
-    made[1].tick(1)
+    made[0].tick(2)
     lax.fori_loop(2, 4, forward, 0)
-    made[0].tick(2)
-    made[2].tick(1)
-    small.tick(2)
+    made[1].tick(2)
+    made[2].tick(2)
+    small.tick(3)
+    loads[2].wait()
     loads[3].wait()
-    loads[4].wait()
     own.wait()
+    made[0].tick(3)
     backward(place.seq)
-    made[1].tick(2)
-    made[0].tick(3)
-    small.tick(3)
     for j in range(3):
         swaps[j].wait_send()
     swaps[2].wait_recv()
     backward((place.seq + 1) % 4)
-    made[2].tick(2)
     made[1].tick(3)
+    made[2].tick(3)
     swaps[1].wait_recv()
-    backward((place.seq + 2) % 4)
-    made[2].tick(3)
     swaps[0].wait_recv()
-    backward((place.seq + 3) % 4)
+    lax.fori_loop(2, 4, lambda j, carry: (backward((place.seq + j) % 4), carry)[1], 0)
     total = small.tick(4)
     for piece in made:
         piece.tick(4)
@@ -877,7 +919,7 @@
         ig_out(r).wait()
 
 
-def finish(dat, heads, gq, go, inp, cot, y, dn, wo, partners, gain, dbias, sums_ff, sums_at, ub, early):
+def finish(dat, heads, gq, go, inp, cot, act, wd, dn, wo, partners, gain, dbias, sums_ff, sums_at, ub, early):
     sd, vm = jax.ShapeDtypeStruct, pltpu.VMEM
     shape, d = inp.shape, inp.shape[2]
     vmem = pl.BlockSpec(memory_space=pltpu.VMEM)
@@ -885,42 +927,45 @@
         tail_kernel,
         out_shape=[sd(shape, BF16), sd(shape, F32), sd((128, 768), F32), sd((128, 256), F32), sd((1, d), F32), sd((1, d), F32), sd((1, 4 * d), F32),
                    sd((1, d), F32)],
-        in_specs=[ANYWHERE] * 9 + [pl.BlockSpec(memory_space=pltpu.SMEM)] + [vmem] * 6, out_specs=[ANYWHERE] * 2 + [vmem] * 6,
+        in_specs=[ANYWHERE] * 10 + [pl.BlockSpec(memory_space=pltpu.SMEM)] + [vmem] * 6, out_specs=[ANYWHERE] * 2 + [vmem] * 6,
         scratch_shapes=[vm(shape, BF16)] * 4 + [vm(shape, F32)] * 2 + [vm((d, d), BF16), vm(shape, BF16), vm(shape, F32),
-                        vm((8, d), F32), vm((3, 8, d), F32), vm((4, 8, d), F32),
-                        DMA((5,)), DMA((8,)), DMA((3,)), DMA((3,)), DMA((1,)), DMA((6,)), DMA((6,)), DMA((4,)), DMA((4,))]
+                        vm((8, d), F32), vm((3, 8, d), F32), vm((4, 8, d), F32), vm((2, 1024, 512), BF16), vm((2, 512, d), BF16), DMA((2,)), DMA((2, 4)),
+                        DMA((4,)), DMA((8,)), DMA((3,)), DMA((3,)), DMA((1,)), DMA((6,)), DMA((6,)), DMA((4,)), DMA((4,))]
         + piece_scratch(256, TAIL_SPLITS[0]) + piece_scratch(384, TAIL_SPLITS[1]) + piece_scratch(384, TAIL_SPLITS[2]),
         compiler_params=pltpu.CompilerParams(collective_id=2, has_side_effects=True, vmem_limit_bytes=56 * 2**20),
-    )(dat.reshape(shape), heads, gq, go, inp, cot, y.reshape(shape), dn.reshape(shape), wo, partners, gain.reshape(1, d), dbias.reshape(1, d), sums_ff, sums_at,
+    )(dat.reshape(shape), heads, gq, go, inp, cot, act, wd, dn.reshape(shape), wo, partners, gain.reshape(1, d), dbias.reshape(1, d), sums_ff, sums_at,
       ub, early)
 
 
-def copy_kernel(*refs):
-    (lo, ig, qkv, out, gain, shift, ub, db), ups, downs = refs[:8], refs[8:12], refs[12:16]
-    lo_o, ig_o, qkv_o, out_o, gain_o, shift_o, ub_o, db_o, up_o, down_o = refs[16:]
-    lo_o[...] = lo[...]
-    ig_o[...] = ig[...]
-
-    @pl.when(pl.program_id(0) == 0)
-    def _():
-        for to, source in ((qkv_o, qkv), (out_o, out), (gain_o, gain), (shift_o, shift), (ub_o, ub), (db_o, db)):
-            to[...] = source[...]
-        for k in range(4):
-            up_o[:, k * 128:(k + 1) * 128] = ups[k][:, 0:128]
-            up_o[:, 512 + k * 128:512 + (k + 1) * 128] = ups[k][:, 128:256]
-            down_o[k * 128:(k + 1) * 128, :] = downs[k][...]
+def copy_kernel(*refs, moves, count):
+    ins, outs, held, (in_sem, out_sem) = refs[:count], refs[count:count + 10], refs[count + 10:2 * count + 10], refs[2 * count + 10:]
+    loads = [local_copy(ins[a].at[at], held[a].at[at], in_sem.at[k]) for k, (a, at, _) in enumerate(moves)]
+    for copy in loads:
+        copy.start()
+    stores = []
+    for k, (a, at, places) in enumerate(moves):
+        loads[k].wait()
+        for source, b, to in places:
+            stores.append(local_copy(held[a].at[source], outs[b].at[to], out_sem.at[len(stores)]))
+            stores[-1].start()
+    for copy in stores:
+        copy.wait()
 
 
 def gather_up(*parts):
-    sd, shape = jax.ShapeDtypeStruct, parts[0].shape
-    flat = [(shape[0] * shape[1], shape[2])] * 2 + [p.shape for p in parts[2:]]
-    band = pl.BlockSpec((128, shape[2]), lambda p: (p, 0))
-    outs = flat[:8] + [(128, 1024), (512, 256)]
+    sd, every = jax.ShapeDtypeStruct, (slice(None), slice(None))
+    shapes = [sd(p.shape, p.dtype) for p in parts[:8]] + [sd((128, 1024), F32), sd((512, 256), F32)]
+    moves = [(a, r, [(r, a, r)]) for r in range(4) for a in (1, 0)]
+    for k in range(4):
+        moves.append((8 + k, every, [((slice(None), slice(half * 128, half * 128 + 128)), 8, (slice(None), slice(half * 512 + k * 128, half * 512 + k * 128 + 128)))
+                                     for half in range(2)]))
+        moves.append((12 + k, every, [(every, 9, (slice(k * 128, k * 128 + 128), slice(None)))]))
+    moves += [(a, every, [(every, a, every)]) for a in range(2, 8)]
     return pl.pallas_call(
-        copy_kernel, out_shape=[sd(s, BF16 if k == 0 else F32) for k, s in enumerate(outs)], grid=(flat[0][0] // 128,),
-        in_specs=[band, band] + [whole(s) for s in flat[2:]], out_specs=[band, band] + [whole(s) for s in outs[2:]],
+        functools.partial(copy_kernel, moves=moves, count=len(parts)), out_shape=shapes, in_specs=[ANYWHERE] * len(parts), out_specs=[ANYWHERE] * 10,
+        scratch_shapes=[pltpu.VMEM(p.shape, p.dtype) for p in parts] + [DMA((len(moves),)), DMA((sum(len(m[2]) for m in moves),))],
         compiler_params=pltpu.CompilerParams(vmem_limit_bytes=60 * 2**20),
-    )(*[p.reshape(s) for p, s in zip(parts, flat)])
+    )(*parts)
 
 
 def on_device(inputs, norm_gain, norm_shift, qkv_weight, out_weight, up_weight, up_bias, down_weight, down_bias, partners, families, cotangent, linked):
@@ -928,12 +973,12 @@
     tokens = row_count * place_count
     branch_args = norm_gain, norm_shift, qkv_weight, out_weight, families, linked
     if linked:
-        y, dn, sums_ff, ub, grads, row_inputs, row_grad, up0, down0, up1, down1 = feed_forward(
+        act, dn, sums_ff, ub, grads, row_inputs, row_grad, up0, down0 = feed_forward(
             inputs, cotangent, partners, norm_gain, norm_shift, up_bias, up_weight, down_weight, True)
-        dat, sums_at, gq, go, heads, up2, down2, up3, down3, early = attend(
+        dat, sums_at, gq, go, heads, up1, down1, up2, down2, up3, down3, early = attend(
             row_inputs.reshape(tokens, width), row_grad.reshape(tokens, width), *branch_args, grads)
         layer_out, input_grad, qkv_sum, out_sum, gain_sum, shift_sum, ub_sum, db_sum = finish(
-            dat, heads, gq, go, inputs, cotangent, y, dn, out_weight, partners, norm_gain, down_bias, sums_ff, sums_at, ub, early)
+            dat, heads, gq, go, inputs, cotangent, act, down_weight, dn, out_weight, partners, norm_gain, down_bias, sums_ff, sums_at, ub, early)
         layer_out, input_grad, qkv_sum, out_sum, gain_sum, shift_sum, ub_sum, db_sum, up_sum, down_sum = gather_up(
             layer_out, input_grad, qkv_sum, out_sum, gain_sum, shift_sum, ub_sum, db_sum, up0, up1, up2, up3, down0, down1, down2, down3)
         return (layer_out.reshape(inputs.shape), input_grad.reshape(inputs.shape), gain_sum.reshape(width), shift_sum.reshape(width), qkv_sum, out_sum,

time: 244 us -> 232 us (0.951)
  Pallas kernels: 243 us -> 231 us
    pallas_call x1, Pallas kernels: 93.8 us -> 75.6 us  [feed_forward(): pl.pallas_call(functools.partial(ff_kernel, linked=linked), out_shape=out...]
    pallas_call x1, Pallas kernels: 93.7 us -> 98.3 us  [attend(): pl.pallas_call(functools.partial(attn_kernel, linked=linked), out_shape=o...]
    pallas_call x1, Pallas kernels: 46.8 us -> 50.6 us  [finish(): pl.pallas_call(tail_kernel, out_shape=[sd(shape, BF16), sd(shape, F32), s...]
    pallas_call x1, Pallas kernels: 8.95 us -> 6.35 us  [gather_up(): pl.pallas_call(functools.partial(copy_kernel, moves=moves, count=len(part...]
where the time goes in v4:
time: 232 us
  Pallas kernels  231 us (100%)
    pallas_call x1, Pallas kernels, attend(): pl.pallas_call(functools.partial(attn_kernel, linked=linked), out_shape=o...  98.3 us
    pallas_call x1, Pallas kernels, feed_forward(): pl.pallas_call(functools.partial(ff_kernel, linked=linked), out_shape=out...  75.6 us
    pallas_call x1, Pallas kernels, finish(): pl.pallas_call(tail_kernel, out_shape=[sd(shape, BF16), sd(shape, F32), s...  50.6 us
    pallas_call x1, Pallas kernels, gather_up(): pl.pallas_call(functools.partial(copy_kernel, moves=moves, count=len(part...  6.35 us

profile of v4, /device:TPU:0, one launch (start us, length us, event | category | flops | bytes accessed | tf_op | source)
XLA Modules:
  0.0 231.8 jit_solution(14688190309516461516)
XLA Ops:
  0.6 75.6 %shard_map.204 = (bf16[8,1024,512]{2,1,0:T(8,128)(2,1)}, f32[1024,1024]{1,0:T(8,128)}, f32[8,1024]{1,0:T(8,128)}, f32[1,4096]{1,0:T(1,128)}, bf16[4,4,2,256,1024...) custom-call(s32[4]{0:T(128)} %part_ref.3, ...), custom_call_target="tpu_custom_call" | custom-call | flops 51999997952 | bytes 50000000 | tf_op jit(solution)/shard_map/pallas_call | solution.py:418
  76.3 98.3 %shard_map.205 = (bf16[1024,1024]{1,0:T(8,128)(2,1)}, f32[8,1024]{1,0:T(8,128)}, bf16[2,4,2,128,1536]{4,3,2,1,0:T(8,128)(2,1)}, bf16[4,2,128,1024]{3,2,1,0:T(8,1...) custom-call(bf16[1024,1024]{1,0:T(8,128)(2,1)} %bitcast.27, ...), custom_call_target="tpu_custom_call" | custom-call | flops 70000001024 | bytes 30000000 | tf_op jit(solution)/shard_map/pallas_call | solution.py:735
  174.6 50.6 %shard_map.206 = (bf16[4,256,1024]{2,1,0:T(8,128)(2,1)}, f32[4,256,1024]{2,1,0:T(8,128)}, f32[128,768]{1,0:T(8,128)}, f32[128,256]{1,0:T(8,128)}, f32[1,1024]{1,...) custom-call(bf16[4,256,1024]{2,1,0:T(8,128)(2,1)} %bitcast.15, ...), custom_call_target="tpu_custom_call" | custom-call | tf_op jit(solution)/shard_map/pallas_call | solution.py:926
  225.3 6.3 %shard_map.207 = (bf16[4,256,1024]{2,1,0:T(8,128)(2,1)}, f32[4,256,1024]{2,1,0:T(8,128)}, f32[128,768]{1,0:T(8,128)}, f32[128,256]{1,0:T(8,128)}, f32[1,1024]{1,...) custom-call(bf16[4,256,1024]{2,1,0:T(8,128)(2,1)} %get-tuple-element, ...), custom_call_target="tpu_custom_call" | custom-call | tf_op jit(solution)/shard_map/pallas_call | solution.py:964

commit v5 on v4

--- a/solution.py
+++ b/solution.py
@@ -88,10 +88,11 @@
         self.partners = [self.twin, self.beside_y, self.beside_x] + self.along_z
 
     def greet(self):
-        barrier = pltpu.get_barrier_semaphore()
         for partner in self.partners + [self.across]:
-            pl.semaphore_signal(barrier, inc=1, device_id=partner, device_id_type=MESH_ID)
-        pl.semaphore_wait(barrier, len(self.partners) + 1)
+            pl.semaphore_signal(pltpu.get_barrier_semaphore(), inc=1, device_id=partner, device_id_type=MESH_ID)
+
+    def meet(self):
+        pl.semaphore_wait(pltpu.get_barrier_semaphore(), len(self.partners) + 1)
 
 
 def add_into(dst, src, lead):
@@ -302,13 +303,12 @@
             copy.start()
         if linked:
             place.greet()
-            for copy in swaps(0):
-                copy.start()
         count, span, _ = cot_ref.shape
         for r in range(count):
             g_ref[r * span:(r + 1) * span, :] = cot_ref[lax.rem(part_ref[r], count)]
         if linked:
-            for copy in swaps(1):
+            place.meet()
+            for copy in swaps(0) + swaps(1):
                 copy.start()
         sums_ref[...] = jnp.zeros_like(sums_ref)
 
@@ -531,16 +531,6 @@
             copy.start()
         if linked:
             place.greet()
-
-    @pl.when(step > 0)
-    def _():
-        for copy in results(step - 1):
-            copy.wait()
-
-    tick(0)
-
-    @pl.when(step == 0)
-    def _():
         family = fam_ref[pl.ds(lax.axis_index("seq"), 1), :].astype(F32)
         famr_s[...] = family
         for m in range(n // 128):
@@ -561,6 +551,15 @@
             normed = (xhat * gain_ref[...] + shift_ref[...]).astype(BF16)
             x_s[rows, :] = normed
             xt_s[:, rows] = normed.T
+        if linked:
+            place.meet()
+
+    @pl.when(step > 0)
+    def _():
+        for copy in results(step - 1):
+            copy.wait()
+
+    tick(0)
 
     @pl.when(step < last)
     def _():
@@ -813,6 +812,7 @@
     small_s[3:4, :] = jnp.zeros((1, d), F32)
     for k in range(4):
         small_s[4 + k:5 + k, :] = ub_ref[:, k * d:(k + 1) * d]
+    place.meet()
     for piece in made:
         piece.tick(0)
     for copy in swaps:

time: 232 us -> 230 us (level)
  no operation moved by 1% of the time
where the time goes in v5:
time: 230 us; the launch traced here: 229 us
  Pallas kernels  229 us (100%)
    pallas_call x1, Pallas kernels, attend(): pl.pallas_call(functools.partial(attn_kernel, linked=linked), out_shape=o...  96.2 us
    pallas_call x1, Pallas kernels, feed_forward(): pl.pallas_call(functools.partial(ff_kernel, linked=linked), out_shape=out...  75.5 us
    pallas_call x1, Pallas kernels, finish(): pl.pallas_call(tail_kernel, out_shape=[sd(shape, BF16), sd(shape, F32), s...  50.5 us
    pallas_call x1, Pallas kernels, gather_up(): pl.pallas_call(functools.partial(copy_kernel, moves=moves, count=len(part...  6.35 us

profile of v5, /device:TPU:0, one launch (start us, length us, event | category | flops | bytes accessed | tf_op | source)
XLA Modules:
  0.0 229.4 jit_solution(10241771548687420181)
XLA Ops:
  0.6 75.5 %shard_map.204 = (bf16[8,1024,512]{2,1,0:T(8,128)(2,1)}, f32[1024,1024]{1,0:T(8,128)}, f32[8,1024]{1,0:T(8,128)}, f32[1,4096]{1,0:T(1,128)}, bf16[4,4,2,256,1024...) custom-call(s32[4]{0:T(128)} %part_ref.3, ...), custom_call_target="tpu_custom_call" | custom-call | flops 51999997952 | bytes 50000000 | tf_op jit(solution)/shard_map/pallas_call | solution.py:418
  76.1 96.2 %shard_map.205 = (bf16[1024,1024]{1,0:T(8,128)(2,1)}, f32[8,1024]{1,0:T(8,128)}, bf16[2,4,2,128,1536]{4,3,2,1,0:T(8,128)(2,1)}, bf16[4,2,128,1024]{3,2,1,0:T(8,1...) custom-call(bf16[1024,1024]{1,0:T(8,128)(2,1)} %bitcast.27, ...), custom_call_target="tpu_custom_call" | custom-call | flops 70000001024 | bytes 30000000 | tf_op jit(solution)/shard_map/pallas_call | solution.py:734
  172.3 50.5 %shard_map.206 = (bf16[4,256,1024]{2,1,0:T(8,128)(2,1)}, f32[4,256,1024]{2,1,0:T(8,128)}, f32[128,768]{1,0:T(8,128)}, f32[128,256]{1,0:T(8,128)}, f32[1,1024]{1,...) custom-call(bf16[4,256,1024]{2,1,0:T(8,128)(2,1)} %bitcast.15, ...), custom_call_target="tpu_custom_call" | custom-call | tf_op jit(solution)/shard_map/pallas_call | solution.py:926
  222.8 6.3 %shard_map.207 = (bf16[4,256,1024]{2,1,0:T(8,128)(2,1)}, f32[4,256,1024]{2,1,0:T(8,128)}, f32[128,768]{1,0:T(8,128)}, f32[128,256]{1,0:T(8,128)}, f32[1,1024]{1,...) custom-call(bf16[4,256,1024]{2,1,0:T(8,128)(2,1)} %get-tuple-element, ...), custom_call_target="tpu_custom_call" | custom-call | tf_op jit(solution)/shard_map/pallas_call | solution.py:964

commit v6 on v5

--- a/solution.py
+++ b/solution.py
@@ -812,12 +812,6 @@
     small_s[3:4, :] = jnp.zeros((1, d), F32)
     for k in range(4):
         small_s[4 + k:5 + k, :] = ub_ref[:, k * d:(k + 1) * d]
-    place.meet()
-    for piece in made:
-        piece.tick(0)
-    for copy in swaps:
-        copy.start()
-    small.tick(0)
     loads = [local_copy(a, b, load_sem.at[k]) for k, (a, b) in enumerate(
         ((heads_ref, heads_s), (inp_ref, inp_s), (cot_ref, g_s), (dn_ref, dn_s)))]
     for pair in range(d // 128):
@@ -825,6 +819,12 @@
         blocks[at] = local_copy(wo_ref.at[pl.ds(pair * 128, 128), :], wo_s.at[pl.ds(at * 128, 128), :], wo_sem.at[at])
     for copy in [loads[0]] + list(blocks.values()) + loads[1:] + [own]:
         copy.start()
+    place.meet()
+    for piece in made:
+        piece.tick(0)
+    for copy in swaps:
+        copy.start()
+    small.tick(0)
 
     def lo_out(r):
         return local_copy(lo_s.at[r], lo_ref.at[r], lo_sem.at[r])

time: 230 us -> 230 us (level)
  no operation moved by 1% of the time
where the time goes in v6:
time: 230 us; the launch traced here: 229 us
  Pallas kernels  229 us (100%)
    pallas_call x1, Pallas kernels, attend(): pl.pallas_call(functools.partial(attn_kernel, linked=linked), out_shape=o...  96.2 us
    pallas_call x1, Pallas kernels, feed_forward(): pl.pallas_call(functools.partial(ff_kernel, linked=linked), out_shape=out...  75.5 us
    pallas_call x1, Pallas kernels, finish(): pl.pallas_call(tail_kernel, out_shape=[sd(shape, BF16), sd(shape, F32), s...  50.5 us
    pallas_call x1, Pallas kernels, gather_up(): pl.pallas_call(functools.partial(copy_kernel, moves=moves, count=len(part...  6.35 us

profile of v6, /device:TPU:0, one launch (start us, length us, event | category | flops | bytes accessed | tf_op | source)
XLA Modules:
  0.0 229.4 jit_solution(15178912156601592149)
XLA Ops:
  0.6 75.5 %shard_map.204 = (bf16[8,1024,512]{2,1,0:T(8,128)(2,1)}, f32[1024,1024]{1,0:T(8,128)}, f32[8,1024]{1,0:T(8,128)}, f32[1,4096]{1,0:T(1,128)}, bf16[4,4,2,256,1024...) custom-call(s32[4]{0:T(128)} %part_ref.3, ...), custom_call_target="tpu_custom_call" | custom-call | flops 51999997952 | bytes 50000000 | tf_op jit(solution)/shard_map/pallas_call | solution.py:418
  76.1 96.2 %shard_map.205 = (bf16[1024,1024]{1,0:T(8,128)(2,1)}, f32[8,1024]{1,0:T(8,128)}, bf16[2,4,2,128,1536]{4,3,2,1,0:T(8,128)(2,1)}, bf16[4,2,128,1024]{3,2,1,0:T(8,1...) custom-call(bf16[1024,1024]{1,0:T(8,128)(2,1)} %bitcast.27, ...), custom_call_target="tpu_custom_call" | custom-call | flops 70000001024 | bytes 30000000 | tf_op jit(solution)/shard_map/pallas_call | solution.py:734
  172.3 50.5 %shard_map.206 = (bf16[4,256,1024]{2,1,0:T(8,128)(2,1)}, f32[4,256,1024]{2,1,0:T(8,128)}, f32[128,768]{1,0:T(8,128)}, f32[128,256]{1,0:T(8,128)}, f32[1,1024]{1,...) custom-call(bf16[4,256,1024]{2,1,0:T(8,128)(2,1)} %bitcast.15, ...), custom_call_target="tpu_custom_call" | custom-call | tf_op jit(solution)/shard_map/pallas_call | solution.py:926
  222.8 6.3 %shard_map.207 = (bf16[4,256,1024]{2,1,0:T(8,128)(2,1)}, f32[4,256,1024]{2,1,0:T(8,128)}, f32[128,768]{1,0:T(8,128)}, f32[128,256]{1,0:T(8,128)}, f32[1,1024]{1,...) custom-call(bf16[4,256,1024]{2,1,0:T(8,128)(2,1)} %get-tuple-element, ...), custom_call_target="tpu_custom_call" | custom-call | tf_op jit(solution)/shard_map/pallas_call | solution.py:964
